TPU v7x, 32 devices: a whole 2x2x4 slice. The times are simulated.
32 devices in a mesh: fsdp: 8 (over y, x, core), tp: 4 (over z).
Axes of the slice: x: 2, y: 2, z: 4, core: 2. Of those that a mesh axis runs over, the one named last changes fastest.
Arguments:
- features: bfloat16 [1024, 8192], P('fsdp'), may hold values from -17 to 17
- key_partials: bfloat16 [1024, 4, 128], P('fsdp', 'tp'), may hold values from -0.30935922 to 0.30935922
- momentum: float32 [4096, 4, 128], P('fsdp', 'tp'), may hold values from -6 to 6
Outputs:
- update: float32 [4096, 4, 128], P('fsdp', 'tp')
- new_momentum: float32 [4096, 4, 128], P('fsdp', 'tp')
All inputs are finite; a program needn't handle non-finite values.
Results may differ from a plain program's by a relative error of at most 0.0003.
Values may be sent and summed in bfloat16 or wider, within the bound.
No kernel may reach another device: no remote copies, remote signals or barrier semaphores. Data moves between devices by JAX's collectives and lax.ppermute only.
A program may use at most 64 MiB of HBM per device.

v0:
```python
import math

import jax
import jax.numpy as jnp
from jax import lax
from jax.sharding import PartitionSpec as P

D_W = 8192
ITERS = 5


retain = 0.95
first_coef = 3.4445
second_coef = -4.775
third_coef = 2.0315
epsilon = 1e-07
shrink = 0.2


def swapped(block, axis, distance):
    count = lax.axis_size(axis)
    route = []
    for low in range(count):
        high = low | 1 << distance
        if high != low and high < count:
            route += [(low, high), (high, low)]
    return lax.ppermute(block, axis, route)


def on_device(features, key_partials, momentum):
    precise = lax.Precision.HIGHEST
    contract = (((0,), (0,)), ((), ()))
    parity = lax.axis_index("tp") % 2
    own_part = key_partials[:, 0, :]
    head_size = key_partials.shape[2]
    rows_half = momentum.shape[0]
    shard = lax.psum_scatter(
        lax.dot_general(features, own_part, contract, preferred_element_type=jnp.float32),
        "fsdp",
        scatter_dimension=0,
        tiled=True,
    )
    pieces = shard.reshape(2, rows_half, head_size)
    mine = jnp.where(parity == 0, pieces[0], pieces[1])
    other = jnp.where(parity == 0, pieces[1], pieces[0])
    grads = mine + swapped(other, "tp", 0)
    moment = momentum[:, 0, :]
    fresh = retain * moment + grads
    blend = grads + retain * fresh
    gram = lax.dot_general(blend, blend, contract, precision=precise)
    gram = lax.psum(gram, "fsdp")
    gram = gram + swapped(gram, "tp", 0)
    inverse = 1.0 / (jnp.sqrt(jnp.trace(gram)) + epsilon)
    state = blend * inverse
    gram = gram * (inverse * inverse)
    identity = jnp.eye(head_size, dtype=jnp.float32)
    for step in range(ITERS):
        square = jnp.dot(gram, gram, precision=precise)
        poly = first_coef * identity + second_coef * gram + third_coef * square
        state = jnp.dot(state, poly, precision=precise)
        gram = jnp.dot(poly, jnp.dot(gram, poly, precision=precise), precision=precise)
    update = shrink * math.sqrt(D_W) * state
    return (update[:, None, :], fresh[:, None, :])


def solution(mesh):
    placed = (P("fsdp", None), P("fsdp", "tp", None), P("fsdp", "tp", None))
    return jax.shard_map(
        on_device,
        mesh=mesh,
        in_specs=placed,
        out_specs=(P("fsdp", "tp", None), P("fsdp", "tp", None)),
        check_vma=False,
    )
```

profile of v0, /device:TPU:0, one launch (start us, length us, event | category | flops | bytes accessed | tf_op | source)
XLA Modules:
  0.0 150.5 jit_solution(14905172062143592151)
XLA Ops:
  7.2 0.0 copy-start
  7.2 0.0 reduce-scatter.2.cloned.1.call-start
  7.2 1.5 %copy-done = bf16[128,8192]{1,0:T(8,128)(2,1)S(1)} copy-done((bf16[128,8192]{1,0:T(8,128)(2,1)S(1)}, bf16[128,8192]{1,0:T(8,128)(2,1)}, u32[]{:S(2)}) %copy-start) | copy-done | bytes 2097176
  8.8 3.4 %fusion.14 = f32[8192,128]{1,0:T(8,128)} fusion(bf16[128,8192]{1,0:T(8,128)(2,1)S(1)} %copy-done, bf16[128,1,128]{2,0,1:T(8,128)(2,1)} %param.4), kind=kOutput, calls=%fused_computation.29 | convolution fusion | flops 268435456 | bytes 6324224 | tf_op jit(solution)/shard_map/dot_general | solution.py:38
  12.2 0.0 copy-start.1
  12.2 0.0 reduce-scatter.2.cloned.1.call-update
  12.2 0.0 all-reduce.2.cloned.1.call-start
  12.3 54.0 %reduce-scatter.2.cloned.1.call-done = f32[1024,128]{1,0:T(8,128)} async-done(((f32[8192,128]{1,0:T(8,128)}), f32[1024,128]{1,0:T(8,128)}) %reduce-scatter.2.cloned.1.call-update) | async-done | bytes 524304 | tf_op jit(solution)/shard_map/reduce_scatter | solution.py:37
  66.3 1.1 slice_select_fusion
  67.3 1.5 %collective-permute-start = (f32[512,128]{1,0:T(8,128)S(1)}, f32[512,128]{1,0:T(8,128)S(1)}, u32[]{:S(2)}, u32[]{:S(2)}) collective-permute-start(f32[512,128]{1,0:T(8,128)S(1)} %slice_select_fusion), channel_id=1, source_target_pairs={{0,1},{1,0},{2,3},{3,2},{4,5},{5,4},{6,7},{7,6},{8,9},{9,8},{10,11... | collective-permute-start | bytes 786440 | tf_op jit(solution)/shard_map/ppermute | solution.py:27
  68.9 6.4 %collective-permute-done = f32[512,128]{1,0:T(8,128)S(1)} collective-permute-done((f32[512,128]{1,0:T(8,128)S(1)}, f32[512,128]{1,0:T(8,128)S(1)}, u32[]{:S(2)}, u32[]{:S(2)}) %collective-permute-start) | collective-permute-done | bytes 262176 | tf_op jit(solution)/shard_map/ppermute | solution.py:27
  75.3 0.0 copy-done.1
  75.3 1.8 %bitcast_add_fusion = (f32[512,128]{1,0:T(8,128)}, f32[512,128]{1,0:T(8,128)S(1)}) fusion(f32[512,1,128]{2,0,1:T(8,128)S(1)} %bitcast.51, f32[512,128]{1,0:T(8,128)S(1)} %collective-permute-done, f32[1024,128]{1,0:T(8,128)} %reduce-scatter.2.cloned.1.call-done, pred[]{:T(512)S(6)} %eq.21), kind=kLoop, calls=%fused_computation.10 | loop fusion | flops 262144 | bytes 1572865 | tf_op jit(solution)/shard_map/add | solution.py:48
  77.1 1.2 fusion.7
  78.3 0.0 all-reduce.2.cloned.1.call-update
  78.3 53.3 %all-reduce.2.cloned.1.call-done = f32[128,128]{1,0:T(8,128)} async-done(((f32[128,128]{1,0:T(8,128)}), f32[128,128]{1,0:T(8,128)}) %all-reduce.2.cloned.1.call-update) | async-done | bytes 65552 | tf_op jit(solution)/shard_map/psum | solution.py:51
  131.7 1.5 collective-permute-start.1
  133.2 3.0 %collective-permute-done.1 = f32[128,128]{1,0:T(8,128)S(1)} collective-permute-done((f32[128,128]{1,0:T(8,128)}, f32[128,128]{1,0:T(8,128)S(1)}, u32[]{:S(2)}, u32[]{:S(2)}) %collective-permute-start.1) | collective-permute-done | bytes 65568 | tf_op jit(solution)/shard_map/ppermute | solution.py:27
  136.2 1.5 select_reduce_fusion
  138.4 0.2 fusion.8
  138.6 0.4 fusion.4
  139.0 0.2 fusion.9
  139.2 0.2 fusion.20
  139.4 0.2 fusion.3
  139.6 0.2 fusion.22
  139.8 0.4 fusion.21
  140.2 0.2 fusion.23
  140.4 0.2 fusion.2
  140.6 0.2 fusion.25
  140.8 0.4 fusion.24
  141.2 0.2 fusion.26
  141.4 0.2 fusion.1
  141.6 0.2 fusion.28
  141.8 0.4 fusion.27
  142.2 0.2 fusion.29
  142.4 0.2 fusion
  142.6 1.1 convolution_multiply_fusion
Async XLA Ops:
  7.2 1.6 %copy-start = (bf16[128,8192]{1,0:T(8,128)(2,1)S(1)}, bf16[128,8192]{1,0:T(8,128)(2,1)}, u32[]{:S(2)}) copy-start(bf16[128,8192]{1,0:T(8,128)(2,1)} %param.3) | copy-start | bytes 6291460
  7.2 59.1 %reduce-scatter.2.cloned.1.call-start = ((), (), s32[]{:S(2)}) async-start(), calls=%async_computation.1 | async-start | bytes 4718592 | tf_op jit(solution)/shard_map/reduce_scatter | solution.py:37
  12.2 63.1 %copy-start.1 = (f32[512,1,128]{2,1,0:T(1,128)S(1)}, f32[512,1,128]{2,1,0:T(1,128)}, u32[]{:S(2)}) copy-start(f32[512,1,128]{2,1,0:T(1,128)} %param.5) | copy-start | bytes 786436
  12.2 119.5 %all-reduce.2.cloned.1.call-start = ((), (), s32[]{:S(2)}) async-start(), calls=%async_computation.2 | async-start | bytes 131072 | tf_op jit(solution)/shard_map/psum | solution.py:51
  67.3 7.9 %collective-permute-start = (f32[512,128]{1,0:T(8,128)S(1)}, f32[512,128]{1,0:T(8,128)S(1)}, u32[]{:S(2)}, u32[]{:S(2)}) collective-permute-start(f32[512,128]{1,0:T(8,128)S(1)} %slice_select_fusion), channel_id=1, source_target_pairs={{0,1},{1,0},{2,3},{3,2},{4,5},{5,4},{6,7},{7,6},{8,9},{9,8},{10,11... | collective-permute-start | bytes 786440 | tf_op jit(solution)/shard_map/ppermute | solution.py:27
  131.7 4.5 %collective-permute-start.1 = (f32[128,128]{1,0:T(8,128)}, f32[128,128]{1,0:T(8,128)S(1)}, u32[]{:S(2)}, u32[]{:S(2)}) collective-permute-start(f32[128,128]{1,0:T(8,128)} %all-reduce.2.cloned.1.call-done), channel_id=1, source_target_pairs={{0,1},{1,0},{2,3},{3,2},{4,5},{5,4},{6,7},{7,6},{8,9},{9,8},{10,11... | collective-permute-start | bytes 196616 | tf_op jit(solution)/shard_map/ppermute | solution.py:27
Sparse Core Ops, SparseCore 0:
  12.4 53.8 reduce-scatter.1
  78.5 53.1 all-reduce.1
where the time goes:
time: 151 us
  waiting for transfers between devices  117 us (77%)
  between operations  14.9 us (10%)
  matrix products  9.86 us (7%)
  other arithmetic  4.35 us (3%)
  starting transfers between devices  3.11 us (2%)
  local copies, waits for them, and re-layouts  1.55 us (1%)
    reduce_scatter x1, waiting for transfers between devices, on_device(): lax.psum_scatter(lax.dot_general(features, own_part, contract, preferred_...  54 us
    psum x1, waiting for transfers between devices, on_device(): gram = lax.psum(gram, 'fsdp')  53.3 us
    ppermute x2, waiting for transfers between devices, swapped(): return lax.ppermute(block, axis, route)  9.37 us
    dot_general x1, matrix products, on_device(): lax.dot_general(features, own_part, contract, preferred_element_type=jnp....  3.45 us
    ppermute x2, starting transfers between devices, swapped(): return lax.ppermute(block, axis, route)  3.03 us
  transfers between devices with their start and end apart: 4, of which 4 were waited for; matrix products, arithmetic and copies ran while one was open for 0% of the time, Pallas kernels for 0%

commit v1 on v0

v1 whole, which is shorter than its diff:
```python
import math

import jax
import jax.numpy as jnp
from jax import lax
from jax.experimental import pallas as pl
from jax.experimental.pallas import tpu as pltpu
from jax.sharding import PartitionSpec as P

ITERS = 5


retain = 0.95
first_coef = 3.4445
second_coef = -4.775
third_coef = 2.0315
epsilon = 1e-07
shrink = 0.2
precise = lax.Precision.HIGHEST
contract = (((0,), (0,)), ((), ()))


def swapped(block, fsdp_bits, tp_bits):
    n_tp = lax.axis_size("tp")
    count = lax.axis_size("fsdp") * n_tp
    mask = fsdp_bits * n_tp + tp_bits
    return lax.ppermute(block, ("fsdp", "tp"), [(i, i ^ mask) for i in range(count)])


def finish(grads, moment_ref, fresh_ref, blend_ref, gram_ref):
    fresh = retain * moment_ref[...] + grads
    blend = grads + retain * fresh
    fresh_ref[...] = fresh
    blend_ref[...] = blend
    gram_ref[...] = lax.dot_general(blend, blend, contract, precision=precise)


def pack_kernel(width, starts_ref, features_ref, *refs):
    outs, sems = refs[:-1], refs[-1]
    copies = []
    for i, out in enumerate(outs):
        for j in range(2):
            start = pl.multiple_of(starts_ref[2 * i + j], width)
            copies.append(
                pltpu.make_async_copy(
                    features_ref.at[:, pl.ds(start, width)],
                    out.at[:, pl.ds(j * width, width)],
                    sems.at[2 * i + j],
                )
            )
    for copy in copies:
        copy.start()
    for copy in copies:
        copy.wait()


def partial_kernel(n_pieces, *refs):
    features, keys = refs[:n_pieces], refs[n_pieces : 2 * n_pieces]
    partner_ref, mine_ref, other_ref = refs[2 * n_pieces :]
    tokens, head_size = keys[0].shape
    grads = None
    for i, (piece, key) in enumerate(zip(features, keys)):
        both = jnp.concatenate([key[...], partner_ref[i * tokens : (i + 1) * tokens, :]], axis=1)
        term = lax.dot_general(both, piece[...], contract, preferred_element_type=jnp.float32)
        grads = term if grads is None else grads + term
    grads = grads[:head_size] + grads[head_size:]
    rows = mine_ref.shape[1]
    mine_ref[...] = grads[:, :rows]
    other_ref[...] = grads[:, rows:]


def joined_kernel(mine_ref, other_ref, moment_ref, fresh_ref, blend_ref, gram_ref):
    finish((mine_ref[...] + other_ref[...]).T, moment_ref, fresh_ref, blend_ref, gram_ref)


def plain_kernel(mine_ref, other_ref, moment_ref, fresh_ref, blend_ref, gram_ref):
    finish(mine_ref[...] + other_ref[...], moment_ref, fresh_ref, blend_ref, gram_ref)


def newton_kernel(scale, n_grams, *refs):
    grams, blend_ref, update_ref = refs[:n_grams], refs[n_grams], refs[n_grams + 1]
    gram = grams[0][...]
    for ref in grams[1:]:
        gram = gram + ref[...]
    size = gram.shape[0]
    rows = lax.broadcasted_iota(jnp.int32, (size, size), 0)
    columns = lax.broadcasted_iota(jnp.int32, (size, size), 1)
    diagonal = rows == columns
    total = jnp.sum(jnp.where(diagonal, gram, 0.0), axis=(0, 1), keepdims=True)
    inverse = 1.0 / (jnp.sqrt(total) + epsilon)
    gram = gram * (inverse * inverse)
    start = jnp.where(diagonal, first_coef, 0.0)
    product = None
    for step in range(ITERS):
        square = jnp.dot(gram, gram, precision=precise)
        poly = start + second_coef * gram + third_coef * square
        product = poly if product is None else jnp.dot(product, poly, precision=precise)
        if step + 1 < ITERS:
            gram = jnp.dot(jnp.dot(gram, poly, precision=precise), poly, precision=precise)
    update_ref[...] = jnp.dot(blend_ref[...] * inverse, product, precision=precise) * scale


def whole(count):
    return [pl.BlockSpec(memory_space=pltpu.VMEM) for _ in range(count)]


def on_device(features, key_partials, momentum):
    n_fsdp = lax.axis_size("fsdp")
    n_tp = lax.axis_size("tp")
    parity = lax.axis_index("tp") % 2
    index = lax.axis_index("fsdp")
    own_part = key_partials[:, 0, :]
    moment = momentum[:, 0, :]
    tokens, head_size = own_part.shape
    rows_half = moment.shape[0]
    bits = [1 << b for b in reversed(range(n_fsdp.bit_length() - 1))]
    direct = n_fsdp == 1 << len(bits) and n_fsdp <= 16 and rows_half % 128 == 0 and n_tp & (n_tp - 1) == 0
    block = jax.ShapeDtypeStruct((rows_half, head_size), jnp.float32)
    small = jax.ShapeDtypeStruct((head_size, head_size), jnp.float32)
    if direct:
        n_chip = n_fsdp // 2
        chip, core = index // 2, index % 2

        def starts_for(distance):
            first = ((chip ^ distance) * 2 + core) * 2 + parity
            second = ((chip ^ distance) * 2 + 1 - core) * 2 + parity
            return [first * rows_half, second * rows_half]

        distances = [d for d in range(n_chip)]
        starts = jnp.stack([s for d in distances for s in starts_for(d)]).astype(jnp.int32)
        packed = jax.ShapeDtypeStruct((tokens, 2 * rows_half), features.dtype)
        pieces = pl.pallas_call(
            lambda *refs: pack_kernel(rows_half, *refs),
            out_shape=(packed,) * n_chip,
            in_specs=[pl.BlockSpec(memory_space=pltpu.SMEM), pl.BlockSpec(memory_space=pl.ANY)],
            out_specs=tuple(whole(n_chip)),
            scratch_shapes=[pltpu.SemaphoreType.DMA((2 * n_chip,))],
            name="pack",
        )(starts, features)
        keys = [own_part if d == 0 else swapped(own_part, 2 * d, 0) for d in distances]
        partner_keys = swapped(jnp.concatenate(keys, axis=0), 0, 1)
        pieces = [pieces[d] if d == 0 else swapped(pieces[d], 2 * d, 0) for d in distances]
        half = jax.ShapeDtypeStruct((head_size, rows_half), jnp.float32)
        mine, other = pl.pallas_call(
            lambda *refs: partial_kernel(n_chip, *refs),
            out_shape=(half, half),
            in_specs=whole(2 * n_chip + 1),
            out_specs=tuple(whole(2)),
            name="partial",
        )(*pieces, *keys, partner_keys)
        fresh, blend, gram = pl.pallas_call(
            joined_kernel,
            out_shape=(block, block, small),
            in_specs=whole(3),
            out_specs=tuple(whole(3)),
            name="gradient",
        )(mine, swapped(other, 1, 0), moment)
        for bit in reversed(bits):
            gram = gram + swapped(gram, bit, 0)
        grams = [gram, swapped(gram, 0, 1)]
    else:
        shard = lax.psum_scatter(
            lax.dot_general(features, own_part, contract, preferred_element_type=jnp.float32),
            "fsdp",
            scatter_dimension=0,
            tiled=True,
        )
        halves = shard.reshape(2, rows_half, head_size)
        mine = jnp.where(parity == 0, halves[0], halves[1])
        other = jnp.where(parity == 0, halves[1], halves[0])
        fresh, blend, gram = pl.pallas_call(
            plain_kernel,
            out_shape=(block, block, small),
            in_specs=whole(3),
            out_specs=tuple(whole(3)),
            name="gradient",
        )(mine, swapped(other, 0, 1), moment)
        gram = lax.psum(gram, "fsdp")
        grams = [gram, swapped(gram, 0, 1)]
    scale = shrink * math.sqrt(2 * n_fsdp * rows_half)
    update = pl.pallas_call(
        lambda *refs: newton_kernel(scale, len(grams), *refs),
        out_shape=block,
        in_specs=whole(len(grams) + 1),
        out_specs=whole(1)[0],
        name="newton",
    )(*grams, blend)
    return (update[:, None, :], fresh[:, None, :])


def solution(mesh):
    placed = (P("fsdp", None), P("fsdp", "tp", None), P("fsdp", "tp", None))
    return jax.shard_map(
        on_device,
        mesh=mesh,
        in_specs=placed,
        out_specs=(P("fsdp", "tp", None), P("fsdp", "tp", None)),
        check_vma=False,
    )
```

time: 151 us -> 53.5 us (0.35)
  waiting for transfers between devices: 117 us -> 20.7 us
  between operations: 14.9 us -> 0.74 us
  Pallas kernels: 0 us -> 13.4 us
  starting transfers between devices: 3.11 us -> 14.8 us
  matrix products: 9.86 us -> 0 us
  other arithmetic: 4.35 us -> 0.88 us
    reduce_scatter x1 -> x0, waiting for transfers between devices: 54 us -> none  [on_device(): lax.psum_scatter(lax.dot_general(features, own_part, contract, preferred_...]
    psum x1 -> x0, waiting for transfers between devices: 53.3 us -> none  [on_device(): gram = lax.psum(gram, 'fsdp')]
    pallas_call x0 -> x4, Pallas kernels: none -> 13.4 us  [the longest x1 5.41 us: on_device(): pl.pallas_call(lambda *refs: newton_kernel(scale, len(grams), *refs), out...]
    ppermute x2 -> x12, starting transfers between devices: 3.03 us -> 14.8 us  [swapped(): lax.ppermute(block, ('fsdp', 'tp'), [(i, i ^ mask) for i in range(count)])]
    ppermute x2 -> x12, waiting for transfers between devices: 9.37 us -> 20.7 us  [swapped(): lax.ppermute(block, ('fsdp', 'tp'), [(i, i ^ mask) for i in range(count)])]
    dot_general x20 -> x0, matrix products: 9.86 us -> none  [the longest x1 3.45 us: on_device(): lax.dot_general(features, own_part, contract, preferred_element_type=jnp....]
  transfers between devices with their start and end apart: 4 -> 12, of which waited for: 4 -> 8; matrix products, arithmetic and copies ran while one was open for 0% -> 1% of each run, Pallas kernels for 0% -> 6%
where the time goes in v1:
time: 53.5 us; the launch traced here: 53.2 us
  waiting for transfers between devices  20.7 us (39%)
  starting transfers between devices  14.8 us (28%)
  Pallas kernels  13.4 us (25%)
  local copies, waits for them, and re-layouts  2.74 us (5%)
  other arithmetic  0.88 us (2%)
  between operations  0.74 us (1%)
    ppermute x12, waiting for transfers between devices, swapped(): lax.ppermute(block, ('fsdp', 'tp'), [(i, i ^ mask) for i in range(count)])  20.7 us
    ppermute x12, starting transfers between devices, swapped(): lax.ppermute(block, ('fsdp', 'tp'), [(i, i ^ mask) for i in range(count)])  14.8 us
    pallas_call x1, Pallas kernels, on_device(): pl.pallas_call(lambda *refs: newton_kernel(scale, len(grams), *refs), out...  5.41 us
    pallas_call x1, Pallas kernels, on_device(): pl.pallas_call(lambda *refs: pack_kernel(rows_half, *refs), out_shape=(pa...  2.98 us
    pallas_call x1, Pallas kernels, on_device(): pl.pallas_call(lambda *refs: partial_kernel(n_chip, *refs), out_shape=(ha...  2.77 us
    pallas_call x1, Pallas kernels, on_device(): pl.pallas_call(joined_kernel, out_shape=(block, block, small), in_specs=w...  2.24 us
    unnamed x22, local copies, waits for them, and re-layouts  2.07 us
  transfers between devices with their start and end apart: 12, of which 8 were waited for; matrix products, arithmetic and copies ran while one was open for 1% of the time, Pallas kernels for 6%

profile of v1, /device:TPU:0, one launch (start us, length us, event | category | flops | bytes accessed | tf_op | source)
XLA Modules:
  0.0 53.2 jit_solution(13576752569221582755)
XLA Ops:
  0.6 0.0 copy-start.6
  0.6 4.0 %collective-permute-start.5 = (bf16[128,128]{1,0:T(8,128)(2,1)}, bf16[128,128]{1,0:T(8,128)(2,1)S(1)}, u32[]{:S(2)}, u32[]{:S(2)}) collective-permute-start(bf16[128,128]{1,0:T(8,128)(2,1)} %bitcast.18), channel_id=1, source_target_pairs={{0,24},{1,25},{2,26},{3,27},{4,28},{5,29},{6,30},{7,31},{8,16},{9,... | collective-permute-start | bytes 98312 | tf_op jit(solution)/shard_map/ppermute | solution.py:27
  4.6 0.5 collective-permute-start.4
  5.1 0.1 collective-permute-start.3
  5.3 0.7 %stack.35.refs_0_ = s32[8]{0:T(128)} concatenate(s32[1]{0:T(128)} %bitcast, s32[1]{0:T(128)} %bitcast.1, s32[1]{0:T(128)} %bitcast.2, s32[1]{0:T(128)} %bitcast.3, s32[1]{0:T(128)} %bitcast.4, s32[1]{0:T(128)} %bitcast.5, s32[1]{0:T(128)} %bitcast.6, s32[1]{0:T(128)} %bitcast.7), dimensions={0} | concatenate | bytes 64 | tf_op jit(solution)/shard_map/stack | solution.py:130
  5.9 3.0 %pack.1 = (bf16[128,1024]{1,0:T(8,128)(2,1)}, bf16[128,1024]{1,0:T(8,128)(2,1)}, bf16[128,1024]{1,0:T(8,128)(2,1)}, bf16[128,1024]{1,0:T(8,128)(2,1)}) custom-call(s32[8]{0:T(128)} %stack.35.refs_0_, bf16[128,8192]{1,0:T(8,128)(2,1)} %refs_1_.1), custom_call_target="tpu_custom_call" | custom-call | tf_op jit(solution)/shard_map/pack/pallas_call | solution.py:132
  8.9 2.0 %collective-permute-start = (bf16[128,1024]{1,0:T(8,128)(2,1)}, bf16[128,1024]{1,0:T(8,128)(2,1)S(1)}, u32[]{:S(2)}, u32[]{:S(2)}) collective-permute-start(bf16[128,1024]{1,0:T(8,128)(2,1)} %get-tuple-element.12), channel_id=1, source_target_pairs={{0,8},{1,9},{2,10},{3,11},{4,12},{5,13},{6,14},{7,15},{8,0},{9,1},... | collective-permute-start | bytes 786440 | tf_op jit(solution)/shard_map/ppermute | solution.py:27
  10.9 1.5 %collective-permute-start.1 = (bf16[128,1024]{1,0:T(8,128)(2,1)}, bf16[128,1024]{1,0:T(8,128)(2,1)S(1)}, u32[]{:S(2)}, u32[]{:S(2)}) collective-permute-start(bf16[128,1024]{1,0:T(8,128)(2,1)} %get-tuple-element.13), channel_id=1, source_target_pairs={{0,16},{1,17},{2,18},{3,19},{4,20},{5,21},{6,22},{7,23},{8,24},{9,... | collective-permute-start | bytes 786440 | tf_op jit(solution)/shard_map/ppermute | solution.py:27
  12.4 0.0 collective-permute-done.5.refs_7_
  12.4 0.0 copy-start.7
  12.4 0.1 collective-permute-start.2
  12.5 0.0 collective-permute-done.4.refs_6_
  12.5 0.0 copy-start.8
  12.5 0.0 collective-permute-done.3.refs_5_
  12.5 0.0 copy-done.6
  12.5 0.0 copy-start.9
  12.5 2.0 %collective-permute-start.6 = (bf16[512,128]{1,0:T(8,128)(2,1)S(1)}, bf16[512,128]{1,0:T(8,128)(2,1)S(1)}, u32[]{:S(2)}, u32[]{:S(2)}) collective-permute-start(bf16[512,128]{1,0:T(8,128)(2,1)S(1)} %pad_maximum_fusion), channel_id=1, source_target_pairs={{0,1},{1,0},{2,3},{3,2},{4,5},{5,4},{6,7},{7,6},{8,9},{9,8},{10,11... | collective-permute-start | bytes 393224 | tf_op jit(solution)/shard_map/ppermute | solution.py:27
  14.6 3.0 %collective-permute-done.6.refs_8_ = bf16[512,128]{1,0:T(8,128)(2,1)S(1)} collective-permute-done((bf16[512,128]{1,0:T(8,128)(2,1)S(1)}, bf16[512,128]{1,0:T(8,128)(2,1)S(1)}, u32[]{:S(2)}, u32[]{:S(2)}) %collective-permute-start.6) | collective-permute-done | bytes 131104 | tf_op jit(solution)/shard_map/ppermute | solution.py:27
  17.6 0.0 copy-start.5
  17.6 0.8 %collective-permute-done.refs_1_ = bf16[128,1024]{1,0:T(8,128)(2,1)S(1)} collective-permute-done((bf16[128,1024]{1,0:T(8,128)(2,1)}, bf16[128,1024]{1,0:T(8,128)(2,1)S(1)}, u32[]{:S(2)}, u32[]{:S(2)}) %collective-permute-start) | collective-permute-done | bytes 262176 | tf_op jit(solution)/shard_map/ppermute | solution.py:27
  18.4 0.0 copy-start
  18.4 5.2 %collective-permute-done.1.refs_2_ = bf16[128,1024]{1,0:T(8,128)(2,1)S(1)} collective-permute-done((bf16[128,1024]{1,0:T(8,128)(2,1)}, bf16[128,1024]{1,0:T(8,128)(2,1)S(1)}, u32[]{:S(2)}, u32[]{:S(2)}) %collective-permute-start.1) | collective-permute-done | bytes 262176 | tf_op jit(solution)/shard_map/ppermute | solution.py:27
  23.6 0.0 collective-permute-done.2.refs_3_
  23.6 0.0 copy-done.7
  23.7 0.0 copy-done.8
  23.7 0.0 copy-done.9
  23.7 0.0 copy-done.5
  23.7 0.0 copy-done
  23.7 0.7 %copy-done.1 = bf16[128,1024]{1,0:T(8,128)(2,1)} copy-done((bf16[128,1024]{1,0:T(8,128)(2,1)}, bf16[128,1024]{1,0:T(8,128)(2,1)S(1)}, u32[]{:S(2)}) %copy-start.1) | copy-done | bytes 262168
  24.3 0.1 copy-done.2
  24.4 2.8 %partial.1 = (f32[128,512]{1,0:T(8,128)}, f32[128,512]{1,0:T(8,128)}) custom-call(bf16[128,1024]{1,0:T(8,128)(2,1)} %get-tuple-element.11.refs_0_, bf16[128,1024]{1,0:T(8,128)(2,1)} %copy-done, bf16[128,1024]{1,0:T(8,128)(2,1)} %copy-done.1, bf16[128,1024]{1,0:T(8,128)(2,1)} %copy-done.2, bf16[128,128]{1,0:T(8,128)(2,1)} %bitcast.21, ...), custom_call_target="tpu_custom_call" | custom-call | tf_op jit(solution)/shard_map/partial/pallas_call | solution.py:144
  27.2 0.0 collective-permute-start.7
  27.2 1.7 %collective-permute-done.7.other_ref = f32[128,512]{1,0:T(8,128)S(1)} collective-permute-done((f32[128,512]{1,0:T(8,128)}, f32[128,512]{1,0:T(8,128)S(1)}, u32[]{:S(2)}, u32[]{:S(2)}) %collective-permute-start.7) | collective-permute-done | bytes 262176 | tf_op jit(solution)/shard_map/ppermute | solution.py:27
  28.9 0.7 %copy-done.3 = f32[128,512]{1,0:T(8,128)} copy-done((f32[128,512]{1,0:T(8,128)}, f32[128,512]{1,0:T(8,128)S(1)}, u32[]{:S(2)}) %copy-start.3) | copy-done | bytes 262168
  29.6 2.2 %gradient.1 = (f32[512,128]{1,0:T(8,128)}, f32[512,128]{1,0:T(8,128)}, f32[128,128]{1,0:T(8,128)}) custom-call(f32[128,512]{1,0:T(8,128)} %get-tuple-element.15.mine_ref, f32[128,512]{1,0:T(8,128)} %copy-done.3, f32[512,128]{1,0:T(8,128)} %bitcast.16), custom_call_target="tpu_custom_call" | custom-call | tf_op jit(solution)/shard_map/gradient/pallas_call | solution.py:151
  31.9 0.1 collective-permute-start.8
  32.0 1.3 %collective-permute-done.8 = f32[128,128]{1,0:T(8,128)S(1)} collective-permute-done((f32[128,128]{1,0:T(8,128)}, f32[128,128]{1,0:T(8,128)S(1)}, u32[]{:S(2)}, u32[]{:S(2)}) %collective-permute-start.8) | collective-permute-done | bytes 65568 | tf_op jit(solution)/shard_map/ppermute | solution.py:27
  33.3 0.9 %add.83 = f32[128,128]{1,0:T(8,128)S(1)} add(f32[128,128]{1,0:T(8,128)} %get-tuple-element.17, f32[128,128]{1,0:T(8,128)S(1)} %collective-permute-done.8) | non-fusion elementwise | flops 16384 | bytes 196608 | tf_op jit(solution)/shard_map/add | solution.py:159
  34.2 1.2 %collective-permute-start.9 = (f32[128,128]{1,0:T(8,128)S(1)}, f32[128,128]{1,0:T(8,128)S(1)}, u32[]{:S(2)}, u32[]{:S(2)}) collective-permute-start(f32[128,128]{1,0:T(8,128)S(1)} %add.83), channel_id=1, source_target_pairs={{0,8},{1,9},{2,10},{3,11},{4,12},{5,13},{6,14},{7,15},{8,0},{9,1},... | collective-permute-start | bytes 196616 | tf_op jit(solution)/shard_map/ppermute | solution.py:27
  35.4 3.1 %collective-permute-done.9 = f32[128,128]{1,0:T(8,128)S(1)} collective-permute-done((f32[128,128]{1,0:T(8,128)S(1)}, f32[128,128]{1,0:T(8,128)S(1)}, u32[]{:S(2)}, u32[]{:S(2)}) %collective-permute-start.9) | collective-permute-done | bytes 65568 | tf_op jit(solution)/shard_map/ppermute | solution.py:27
  38.5 1.6 %collective-permute-start.10 = (f32[128,128]{1,0:T(8,128)S(1)}, f32[128,128]{1,0:T(8,128)S(1)}, u32[]{:S(2)}, u32[]{:S(2)}) collective-permute-start(f32[128,128]{1,0:T(8,128)S(1)} %add.84), channel_id=1, source_target_pairs={{0,16},{1,17},{2,18},{3,19},{4,20},{5,21},{6,22},{7,23},{8,24},{9,... | collective-permute-start | bytes 196616 | tf_op jit(solution)/shard_map/ppermute | solution.py:27
  40.1 2.8 %collective-permute-done.10 = f32[128,128]{1,0:T(8,128)S(1)} collective-permute-done((f32[128,128]{1,0:T(8,128)S(1)}, f32[128,128]{1,0:T(8,128)S(1)}, u32[]{:S(2)}, u32[]{:S(2)}) %collective-permute-start.10) | collective-permute-done | bytes 65568 | tf_op jit(solution)/shard_map/ppermute | solution.py:27
  42.9 0.0 copy-start.4
  42.9 1.6 %collective-permute-start.11 = (f32[128,128]{1,0:T(8,128)S(1)}, f32[128,128]{1,0:T(8,128)S(1)}, u32[]{:S(2)}, u32[]{:S(2)}) collective-permute-start(f32[128,128]{1,0:T(8,128)S(1)} %add.85.refs_0_), channel_id=1, source_target_pairs={{0,1},{1,0},{2,3},{3,2},{4,5},{5,4},{6,7},{7,6},{8,9},{9,8},{10,11... | collective-permute-start | bytes 196616 | tf_op jit(solution)/shard_map/ppermute | solution.py:27
  44.5 2.7 %collective-permute-done.11.refs_1_ = f32[128,128]{1,0:T(8,128)S(1)} collective-permute-done((f32[128,128]{1,0:T(8,128)S(1)}, f32[128,128]{1,0:T(8,128)S(1)}, u32[]{:S(2)}, u32[]{:S(2)}) %collective-permute-start.11) | collective-permute-done | bytes 65568 | tf_op jit(solution)/shard_map/ppermute | solution.py:27
  47.2 0.0 copy-done.4
  47.2 0.6 %copy-done.10 = f32[128,128]{1,0:T(8,128)} copy-done((f32[128,128]{1,0:T(8,128)}, f32[128,128]{1,0:T(8,128)S(1)}, u32[]{:S(2)}) %copy-start.10) | copy-done | bytes 65560
  47.8 5.4 %newton.1 = f32[512,128]{1,0:T(8,128)} custom-call(f32[128,128]{1,0:T(8,128)} %copy-done.4, f32[128,128]{1,0:T(8,128)} %copy-done.10, f32[512,128]{1,0:T(8,128)} %get-tuple-element.18.refs_2_), custom_call_target="tpu_custom_call" | custom-call | tf_op jit(solution)/shard_map/newton/pallas_call | solution.py:181
  (7 shorter events, 0.0 us)
Async XLA Ops:
  0.6 11.9 %copy-start.6 = (bf16[128,1,128]{2,0,1:T(8,128)(2,1)S(1)}, bf16[128,1,128]{2,0,1:T(8,128)(2,1)}, u32[]{:S(2)}) copy-start(bf16[128,1,128]{2,0,1:T(8,128)(2,1)} %param.4) | copy-start | bytes 98308
  0.6 11.8 %collective-permute-start.5 = (bf16[128,128]{1,0:T(8,128)(2,1)}, bf16[128,128]{1,0:T(8,128)(2,1)S(1)}, u32[]{:S(2)}, u32[]{:S(2)}) collective-permute-start(bf16[128,128]{1,0:T(8,128)(2,1)} %bitcast.18), channel_id=1, source_target_pairs={{0,24},{1,25},{2,26},{3,27},{4,28},{5,29},{6,30},{7,31},{8,16},{9,... | collective-permute-start | bytes 98312 | tf_op jit(solution)/shard_map/ppermute | solution.py:27
  4.6 7.9 %collective-permute-start.4 = (bf16[128,128]{1,0:T(8,128)(2,1)}, bf16[128,128]{1,0:T(8,128)(2,1)S(1)}, u32[]{:S(2)}, u32[]{:S(2)}) collective-permute-start(bf16[128,128]{1,0:T(8,128)(2,1)} %bitcast.19), channel_id=1, source_target_pairs={{0,16},{1,17},{2,18},{3,19},{4,20},{5,21},{6,22},{7,23},{8,24},{9,... | collective-permute-start | bytes 98312 | tf_op jit(solution)/shard_map/ppermute | solution.py:27
  5.1 7.4 %collective-permute-start.3 = (bf16[128,128]{1,0:T(8,128)(2,1)}, bf16[128,128]{1,0:T(8,128)(2,1)S(1)}, u32[]{:S(2)}, u32[]{:S(2)}) collective-permute-start(bf16[128,128]{1,0:T(8,128)(2,1)} %bitcast.20), channel_id=1, source_target_pairs={{0,8},{1,9},{2,10},{3,11},{4,12},{5,13},{6,14},{7,15},{8,0},{9,1},... | collective-permute-start | bytes 98312 | tf_op jit(solution)/shard_map/ppermute | solution.py:27
  8.9 9.5 %collective-permute-start = (bf16[128,1024]{1,0:T(8,128)(2,1)}, bf16[128,1024]{1,0:T(8,128)(2,1)S(1)}, u32[]{:S(2)}, u32[]{:S(2)}) collective-permute-start(bf16[128,1024]{1,0:T(8,128)(2,1)} %get-tuple-element.12), channel_id=1, source_target_pairs={{0,8},{1,9},{2,10},{3,11},{4,12},{5,13},{6,14},{7,15},{8,0},{9,1},... | collective-permute-start | bytes 786440 | tf_op jit(solution)/shard_map/ppermute | solution.py:27
  10.9 12.8 %collective-permute-start.1 = (bf16[128,1024]{1,0:T(8,128)(2,1)}, bf16[128,1024]{1,0:T(8,128)(2,1)S(1)}, u32[]{:S(2)}, u32[]{:S(2)}) collective-permute-start(bf16[128,1024]{1,0:T(8,128)(2,1)} %get-tuple-element.13), channel_id=1, source_target_pairs={{0,16},{1,17},{2,18},{3,19},{4,20},{5,21},{6,22},{7,23},{8,24},{9,... | collective-permute-start | bytes 786440 | tf_op jit(solution)/shard_map/ppermute | solution.py:27
  12.4 11.2 %copy-start.7 = (bf16[128,128]{1,0:T(8,128)(2,1)}, bf16[128,128]{1,0:T(8,128)(2,1)S(1)}, u32[]{:S(2)}) copy-start(bf16[128,128]{1,0:T(8,128)(2,1)S(1)} %collective-permute-done.5.refs_7_) | copy-start | bytes 98308
  12.4 11.2 %collective-permute-start.2 = (bf16[128,1024]{1,0:T(8,128)(2,1)}, bf16[128,1024]{1,0:T(8,128)(2,1)S(1)}, u32[]{:S(2)}, u32[]{:S(2)}) collective-permute-start(bf16[128,1024]{1,0:T(8,128)(2,1)} %get-tuple-element.14), channel_id=1, source_target_pairs={{0,24},{1,25},{2,26},{3,27},{4,28},{5,29},{6,30},{7,31},{8,16},{9,... | collective-permute-start | bytes 786440 | tf_op jit(solution)/shard_map/ppermute | solution.py:27
  12.5 11.2 %copy-start.8 = (bf16[128,128]{1,0:T(8,128)(2,1)}, bf16[128,128]{1,0:T(8,128)(2,1)S(1)}, u32[]{:S(2)}) copy-start(bf16[128,128]{1,0:T(8,128)(2,1)S(1)} %collective-permute-done.4.refs_6_) | copy-start | bytes 98308
  12.5 11.2 %copy-start.9 = (bf16[128,128]{1,0:T(8,128)(2,1)}, bf16[128,128]{1,0:T(8,128)(2,1)S(1)}, u32[]{:S(2)}) copy-start(bf16[128,128]{1,0:T(8,128)(2,1)S(1)} %collective-permute-done.3.refs_5_) | copy-start | bytes 98308
  12.5 5.0 %collective-permute-start.6 = (bf16[512,128]{1,0:T(8,128)(2,1)S(1)}, bf16[512,128]{1,0:T(8,128)(2,1)S(1)}, u32[]{:S(2)}, u32[]{:S(2)}) collective-permute-start(bf16[512,128]{1,0:T(8,128)(2,1)S(1)} %pad_maximum_fusion), channel_id=1, source_target_pairs={{0,1},{1,0},{2,3},{3,2},{4,5},{5,4},{6,7},{7,6},{8,9},{9,8},{10,11... | collective-permute-start | bytes 393224 | tf_op jit(solution)/shard_map/ppermute | solution.py:27
  17.6 6.1 %copy-start.5 = (bf16[512,128]{1,0:T(8,128)(2,1)}, bf16[512,128]{1,0:T(8,128)(2,1)S(1)}, u32[]{:S(2)}) copy-start(bf16[512,128]{1,0:T(8,128)(2,1)S(1)} %collective-permute-done.6.refs_8_) | copy-start | bytes 393220
  18.4 5.3 %copy-start = (bf16[128,1024]{1,0:T(8,128)(2,1)}, bf16[128,1024]{1,0:T(8,128)(2,1)S(1)}, u32[]{:S(2)}) copy-start(bf16[128,1024]{1,0:T(8,128)(2,1)S(1)} %collective-permute-done.refs_1_) | copy-start | bytes 786436
  23.6 0.7 %copy-start.1 = (bf16[128,1024]{1,0:T(8,128)(2,1)}, bf16[128,1024]{1,0:T(8,128)(2,1)S(1)}, u32[]{:S(2)}) copy-start(bf16[128,1024]{1,0:T(8,128)(2,1)S(1)} %collective-permute-done.1.refs_2_) | copy-start | bytes 786436
  23.6 0.8 %copy-start.2 = (bf16[128,1024]{1,0:T(8,128)(2,1)}, bf16[128,1024]{1,0:T(8,128)(2,1)S(1)}, u32[]{:S(2)}) copy-start(bf16[128,1024]{1,0:T(8,128)(2,1)S(1)} %collective-permute-done.2.refs_3_) | copy-start | bytes 786436
  27.2 1.7 %collective-permute-start.7 = (f32[128,512]{1,0:T(8,128)}, f32[128,512]{1,0:T(8,128)S(1)}, u32[]{:S(2)}, u32[]{:S(2)}) collective-permute-start(f32[128,512]{1,0:T(8,128)} %get-tuple-element.16), channel_id=1, source_target_pairs={{0,4},{1,5},{2,6},{3,7},{4,0},{5,1},{6,2},{7,3},{8,12},{9,13},{10,... | collective-permute-start | bytes 786440 | tf_op jit(solution)/shard_map/ppermute | solution.py:27
  28.9 0.7 %copy-start.3 = (f32[128,512]{1,0:T(8,128)}, f32[128,512]{1,0:T(8,128)S(1)}, u32[]{:S(2)}) copy-start(f32[128,512]{1,0:T(8,128)S(1)} %collective-permute-done.7.other_ref) | copy-start | bytes 786436
  31.9 1.5 %collective-permute-start.8 = (f32[128,128]{1,0:T(8,128)}, f32[128,128]{1,0:T(8,128)S(1)}, u32[]{:S(2)}, u32[]{:S(2)}) collective-permute-start(f32[128,128]{1,0:T(8,128)} %get-tuple-element.17), channel_id=1, source_target_pairs={{0,4},{1,5},{2,6},{3,7},{4,0},{5,1},{6,2},{7,3},{8,12},{9,13},{10,... | collective-permute-start | bytes 196616 | tf_op jit(solution)/shard_map/ppermute | solution.py:27
  34.2 4.3 %collective-permute-start.9 = (f32[128,128]{1,0:T(8,128)S(1)}, f32[128,128]{1,0:T(8,128)S(1)}, u32[]{:S(2)}, u32[]{:S(2)}) collective-permute-start(f32[128,128]{1,0:T(8,128)S(1)} %add.83), channel_id=1, source_target_pairs={{0,8},{1,9},{2,10},{3,11},{4,12},{5,13},{6,14},{7,15},{8,0},{9,1},... | collective-permute-start | bytes 196616 | tf_op jit(solution)/shard_map/ppermute | solution.py:27
  38.5 4.3 %collective-permute-start.10 = (f32[128,128]{1,0:T(8,128)S(1)}, f32[128,128]{1,0:T(8,128)S(1)}, u32[]{:S(2)}, u32[]{:S(2)}) collective-permute-start(f32[128,128]{1,0:T(8,128)S(1)} %add.84), channel_id=1, source_target_pairs={{0,16},{1,17},{2,18},{3,19},{4,20},{5,21},{6,22},{7,23},{8,24},{9,... | collective-permute-start | bytes 196616 | tf_op jit(solution)/shard_map/ppermute | solution.py:27
  42.9 4.3 %copy-start.4 = (f32[128,128]{1,0:T(8,128)}, f32[128,128]{1,0:T(8,128)S(1)}, u32[]{:S(2)}) copy-start(f32[128,128]{1,0:T(8,128)S(1)} %add.85.refs_0_) | copy-start | bytes 196612
  42.9 4.3 %collective-permute-start.11 = (f32[128,128]{1,0:T(8,128)S(1)}, f32[128,128]{1,0:T(8,128)S(1)}, u32[]{:S(2)}, u32[]{:S(2)}) collective-permute-start(f32[128,128]{1,0:T(8,128)S(1)} %add.85.refs_0_), channel_id=1, source_target_pairs={{0,1},{1,0},{2,3},{3,2},{4,5},{5,4},{6,7},{7,6},{8,9},{9,8},{10,11... | collective-permute-start | bytes 196616 | tf_op jit(solution)/shard_map/ppermute | solution.py:27
  47.2 0.6 %copy-start.10 = (f32[128,128]{1,0:T(8,128)}, f32[128,128]{1,0:T(8,128)S(1)}, u32[]{:S(2)}) copy-start(f32[128,128]{1,0:T(8,128)S(1)} %collective-permute-done.11.refs_1_) | copy-start | bytes 196612

commit v2 on v1

v2 whole, which is shorter than its diff:
```python
import math

import jax
import jax.numpy as jnp
from jax import lax
from jax.experimental import pallas as pl
from jax.experimental.pallas import tpu as pltpu
from jax.sharding import PartitionSpec as P


ITERS = 5


retain = 0.95
first_coef = 3.4445
second_coef = -4.775
third_coef = 2.0315
epsilon = 1e-07
shrink = 0.2
contract = (((0,), (0,)), ((), ()))


def swapped(block, fsdp_bits, tp_bits):
    n_tp = lax.axis_size("tp")
    count = lax.axis_size("fsdp") * n_tp
    mask = fsdp_bits * n_tp + tp_bits
    return lax.ppermute(block, ("fsdp", "tp"), [(i, i ^ mask) for i in range(count)])


def halves(value):
    high = value.astype(jnp.bfloat16)
    return high, (value - high.astype(jnp.float32)).astype(jnp.bfloat16)


def thirds(value):
    high = value.astype(jnp.bfloat16)
    rest = value - high.astype(jnp.float32)
    middle = rest.astype(jnp.bfloat16)
    return high, middle, (rest - middle.astype(jnp.float32)).astype(jnp.bfloat16)


def product_of(left, right):
    l1, l2, l3 = left
    r1, r2, r3 = right
    columns = r1.shape[1]
    square = jnp.concatenate([jnp.concatenate([r1, r2], 1), jnp.concatenate([r2, r1], 1)], 0)
    main = jnp.dot(jnp.concatenate([l1, l2], 1), square, preferred_element_type=jnp.float32)
    rest = jnp.dot(jnp.concatenate([l1, l3], 1), jnp.concatenate([r3, r1], 0), preferred_element_type=jnp.float32)
    return (rest + main[:, columns:]) + main[:, :columns]


def gram_of(value):
    width = value.shape[1]
    both = jnp.concatenate(halves(value), axis=1)
    parts = lax.dot_general(both, both, contract, preferred_element_type=jnp.float32)
    cross = parts[:width, width:] + parts[width:, :width]
    return (parts[width:, width:] + cross) + parts[:width, :width]


def packed_gram(gram):
    half = gram.shape[0] // 2
    upper, corner = gram[:half], gram[half:, half:]
    shape = (half, half)
    rows, columns = (lax.broadcasted_iota(jnp.int32, shape, axis) for axis in range(2))
    left = jnp.where(rows >= columns, upper[:, :half], corner)
    diagonal = jnp.sum(jnp.where(rows == columns, corner, 0.0), axis=0, keepdims=True)
    diagonal = jnp.broadcast_to(jnp.concatenate([diagonal, diagonal], axis=1), (8, 2 * half))
    return jnp.concatenate([jnp.concatenate([left, upper[:, half:]], axis=1), diagonal], axis=0)


def unpacked_gram(packed):
    half = packed.shape[1] // 2
    left, right, diagonal = packed[:half, :half], packed[:half, half:], packed[half : half + 1, :half]
    rows, columns = (lax.broadcasted_iota(jnp.int32, (half, half), axis) for axis in range(2))
    weight = jnp.where(rows == columns, 0.5, 1.0)
    first = jnp.where(rows >= columns, left * weight, 0.0)
    second = jnp.where(rows < columns, left, jnp.where(rows == columns, 0.5 * diagonal, 0.0))
    top = jnp.concatenate([first, right], axis=1)
    bottom = jnp.concatenate([jnp.zeros((half, half), jnp.float32), second], axis=1)
    triangle = jnp.concatenate([top, bottom], axis=0)
    return triangle + triangle.T


def advanced(grads, moment):
    fresh = retain * moment + grads
    return fresh, grads + retain * fresh


def pack_kernel(width, features_ref, *refs):
    outs, sems = refs[:-1], refs[-1]
    index = lax.axis_index("fsdp")
    parity = lax.axis_index("tp") % 2
    chip, core = index // 2, index % 2
    copies = []
    for i, out in enumerate(outs):
        for j in range(2):
            block = (chip ^ i) * 2 + (core ^ j)
            start = pl.multiple_of((block * 2 + parity) * width, width)
            copies.append(
                pltpu.make_async_copy(
                    features_ref.at[:, pl.ds(start, width)],
                    out.at[:, pl.ds(j * width, width)],
                    sems.at[2 * i + j],
                )
            )
    for copy in copies:
        copy.start()
    for copy in copies:
        copy.wait()


def partial_kernel(n_pieces, *refs):
    features, keys = refs[:n_pieces], refs[n_pieces : 2 * n_pieces]
    partner_ref, grads_ref = refs[2 * n_pieces :]
    head_size = grads_ref.shape[1]
    own = jnp.concatenate([key[...] for key in keys], axis=0)
    keys = jnp.concatenate([own, partner_ref[...]], axis=1)
    features = jnp.concatenate([piece[...] for piece in features], axis=0)
    both = lax.dot_general(features, keys, contract, preferred_element_type=jnp.float32)
    grads_ref[...] = both[:, :head_size] + both[:, head_size:]


def joined_kernel(own_ref, other_ref, moment_ref, twin_ref, fresh_ref, blend_ref, gram_ref):
    rows = moment_ref.shape[0]
    fresh, blend = advanced(own_ref[:rows] + other_ref[rows:], moment_ref[...])
    twin = advanced(own_ref[rows:] + other_ref[:rows], twin_ref[...])[1]
    fresh_ref[...] = fresh
    blend_ref[...] = blend
    gram_ref[...] = packed_gram(gram_of(jnp.concatenate([blend, twin], axis=0)))


def plain_kernel(mine_ref, other_ref, moment_ref, fresh_ref, blend_ref, gram_ref):
    fresh, blend = advanced(mine_ref[...] + other_ref[...], moment_ref[...])
    fresh_ref[...] = fresh
    blend_ref[...] = blend
    gram_ref[...] = packed_gram(gram_of(blend))


def applied(value, factor):
    columns = factor.shape[1]
    left = jnp.concatenate(halves(value), axis=1)
    right = jnp.concatenate(halves(factor), axis=1)
    both = jnp.dot(left, jnp.concatenate([right, right], axis=0), preferred_element_type=jnp.float32)
    return both[:, columns:] + both[:, :columns]


def stacked(first, second):
    return tuple(jnp.concatenate(pair, axis=0) for pair in zip(first, second))


def newton_kernel(scale, n_grams, *refs):
    grams, blend_ref, update_ref, staged_ref, sems = refs[:n_grams], *refs[n_grams:]
    total = grams[0][...]
    for ref in grams[1:]:
        total = total + ref[...]
    gram = unpacked_gram(total)
    size = gram.shape[0]
    rows = lax.broadcasted_iota(jnp.int32, (size, size), 0)
    columns = lax.broadcasted_iota(jnp.int32, (size, size), 1)
    diagonal = rows == columns
    trace = jnp.sum(jnp.where(diagonal, gram, 0.0), axis=(0, 1), keepdims=True)
    inverse = 1.0 / (jnp.sqrt(trace) + epsilon)
    gram = gram * (inverse * inverse)
    start = jnp.where(diagonal, first_coef, 0.0)
    product = None
    for _ in range(ITERS - 1):
        split = thirds(gram)
        square = product_of(split, split)
        poly = start + second_coef * gram + third_coef * square
        factor = thirds(poly)
        if product is None:
            product, turned = poly, product_of(split, factor)
        else:
            both = product_of(stacked(split, thirds(product)), factor)
            turned, product = both[:size], both[size:]
        gram = product_of(thirds(turned), factor)
    split = thirds(gram)
    poly = start + second_coef * gram + third_coef * product_of(split, split)
    partway = applied(blend_ref[...], product * (inverse * scale))
    chunk = partway.shape[0] // 4
    copies = []
    for i in range(4):
        part = pl.ds(i * chunk, chunk)
        staged_ref[part, :] = applied(partway[i * chunk : (i + 1) * chunk], poly)
        copies.append(pltpu.make_async_copy(staged_ref.at[part], update_ref.at[part], sems.at[i]))
        copies[-1].start()
    for copy in copies:
        copy.wait()


def whole(count):
    return [pl.BlockSpec(memory_space=pltpu.VMEM) for _ in range(count)]


def on_chip(*arrays):
    return [pltpu.with_memory_space_constraint(array, pltpu.VMEM) for array in arrays]


def ordered(features, key_partials, momentum):
    n_fsdp = lax.axis_size("fsdp")
    n_tp = lax.axis_size("tp")
    parity = lax.axis_index("tp") % 2
    own_part = key_partials[:, 0, :]
    moment = momentum[:, 0, :]
    tokens, head_size = own_part.shape
    rows_half = moment.shape[0]
    bits = [1 << b for b in reversed(range(n_fsdp.bit_length() - 1))]
    direct = n_fsdp == 1 << len(bits) and n_fsdp <= 16 and rows_half % 128 == 0 and n_tp & (n_tp - 1) == 0
    block = pltpu.VMEM((rows_half, head_size), jnp.float32)
    small = pltpu.VMEM((head_size // 2 + 8, head_size), jnp.float32)
    if direct:
        n_chip = n_fsdp // 2
        packed = pltpu.VMEM((tokens, 2 * rows_half), features.dtype)
        pieces = pl.pallas_call(
            lambda *refs: pack_kernel(rows_half, *refs),
            out_shape=(packed,) * n_chip,
            in_specs=[pl.BlockSpec(memory_space=pl.ANY)],
            out_specs=tuple(whole(n_chip)),
            scratch_shapes=[pltpu.SemaphoreType.DMA((2 * n_chip,))],
            name="pack",
        )(features)
        pieces, own_part = lax.optimization_barrier((pieces, own_part))
        pieces = list(pieces)
        for d in range(1, n_chip):
            pieces[d] = swapped(pieces[d], 2 * d, 0)
        keys = [own_part]
        for d in range(1, n_chip):
            keys.append(swapped(own_part, 2 * d, 0))
        partner_keys = swapped(jnp.concatenate(keys, axis=0), 0, 1)
        twin = swapped(moment, 1, 0)
        partner_keys, twin = lax.optimization_barrier((partner_keys, twin))
        grads = pl.pallas_call(
            lambda *refs: partial_kernel(n_chip, *refs),
            out_shape=pltpu.VMEM((2 * rows_half, head_size), jnp.float32),
            in_specs=whole(2 * n_chip + 1),
            out_specs=whole(1)[0],
            name="partial",
        )(*on_chip(*pieces, *keys, partner_keys))
        fresh, blend, gram = pl.pallas_call(
            joined_kernel,
            out_shape=(block, block, small),
            in_specs=whole(4),
            out_specs=tuple(whole(3)),
            name="gradient",
        )(*on_chip(grads, swapped(grads, 1, 0), moment, twin))
        for bit in bits[:-1]:
            gram = gram + swapped(gram, bit, 0)
        grams = [gram, swapped(gram, 0, 1)]
    else:
        shard = lax.psum_scatter(
            lax.dot_general(features, own_part, contract, preferred_element_type=jnp.float32),
            "fsdp",
            scatter_dimension=0,
            tiled=True,
        )
        pair = shard.reshape(2, rows_half, head_size)
        mine = jnp.where(parity == 0, pair[0], pair[1])
        other = jnp.where(parity == 0, pair[1], pair[0])
        fresh, blend, gram = pl.pallas_call(
            plain_kernel,
            out_shape=(block, block, small),
            in_specs=whole(3),
            out_specs=tuple(whole(3)),
            name="gradient",
        )(*on_chip(mine, swapped(other, 0, 1), moment))
        gram = lax.psum(gram, "fsdp")
        grams = [gram, swapped(gram, 0, 1)]
    scale = shrink * math.sqrt(2 * n_fsdp * rows_half)
    update = pl.pallas_call(
        lambda *refs: newton_kernel(scale, len(grams), *refs),
        out_shape=jax.ShapeDtypeStruct((rows_half, head_size), jnp.float32),
        in_specs=whole(len(grams) + 1),
        out_specs=pl.BlockSpec(memory_space=pl.ANY),
        scratch_shapes=[pltpu.VMEM((rows_half, head_size), jnp.float32), pltpu.SemaphoreType.DMA((4,))],
        name="newton",
    )(*on_chip(*grams, blend))
    return (update[:, None, :], fresh[:, None, :])


def solution(mesh):
    placed = (P("fsdp", None), P("fsdp", "tp", None), P("fsdp", "tp", None))
    return jax.shard_map(
        ordered,
        mesh=mesh,
        in_specs=placed,
        out_specs=(P("fsdp", "tp", None), P("fsdp", "tp", None)),
        check_vma=False,
    )
```

time: 53.5 us -> 41.1 us (0.77)
  Pallas kernels: 13.4 us -> 5.84 us
  waiting for transfers between devices: 20.7 us -> 18.4 us
  local copies, waits for them, and re-layouts: 2.74 us -> 0.71 us
  other arithmetic: 0.88 us -> 0.02 us
    pallas_call x4, Pallas kernels: 13.4 us -> 5.84 us  [the longest x1 3.38 us: ordered(): pl.pallas_call(lambda *refs: newton_kernel(scale, len(grams), *refs), out...]
    ppermute x12, waiting for transfers between devices: 20.7 us -> 18.4 us  [swapped(): lax.ppermute(block, ('fsdp', 'tp'), [(i, i ^ mask) for i in range(count)])]
    unnamed x22 -> x5, local copies, waits for them, and re-layouts: 2.07 us -> 0.71 us
    add x3 -> x2, other arithmetic: 0.87 us -> 0.01 us  [ordered(): gram = gram + swapped(gram, bit, 0)]
    another operation x1 -> x0, local copies, waits for them, and re-layouts: 0.66 us -> none  [on_device(): jnp.stack([s for d in distances for s in starts_for(d)]).astype(jnp.int32)]
    ppermute x12, starting transfers between devices: 14.8 us -> 15.3 us  [swapped(): lax.ppermute(block, ('fsdp', 'tp'), [(i, i ^ mask) for i in range(count)])]
  transfers between devices with their start and end apart: 12 -> 12, of which waited for: 8 -> 7; matrix products, arithmetic and copies ran while one was open for 1% -> 2% of each run, Pallas kernels for 6% -> 0%
where the time goes in v2:
time: 41.1 us; the launch traced here: 41 us
  waiting for transfers between devices  18.4 us (45%)
  starting transfers between devices  15.3 us (37%)
  Pallas kernels  5.84 us (14%)
  local copies, waits for them, and re-layouts  0.71 us (2%)
  between operations  0.69 us (2%)
    ppermute x12, waiting for transfers between devices, swapped(): lax.ppermute(block, ('fsdp', 'tp'), [(i, i ^ mask) for i in range(count)])  18.4 us
    ppermute x12, starting transfers between devices, swapped(): lax.ppermute(block, ('fsdp', 'tp'), [(i, i ^ mask) for i in range(count)])  15.3 us
    pallas_call x1, Pallas kernels, ordered(): pl.pallas_call(lambda *refs: newton_kernel(scale, len(grams), *refs), out...  3.38 us
    pallas_call x1, Pallas kernels, ordered(): pl.pallas_call(lambda *refs: pack_kernel(rows_half, *refs), out_shape=(pa...  1.41 us
  transfers between devices with their start and end apart: 12, of which 7 were waited for; matrix products, arithmetic and copies ran while one was open for 2% of the time, Pallas kernels for 0%

profile of v2, /device:TPU:0, one launch (start us, length us, event | category | flops | bytes accessed | tf_op | source)
XLA Modules:
  0.0 41.0 jit_solution(3532040824588562249)
XLA Ops:
  0.6 0.0 copy-start.1
  0.6 0.0 copy-start
  0.6 1.4 %pack.1 = (bf16[128,1024]{1,0:T(8,128)(2,1)S(1)}, bf16[128,1024]{1,0:T(8,128)(2,1)S(1)}, bf16[128,1024]{1,0:T(8,128)(2,1)S(1)}, bf16[128,1024]{1,0:T(8,128)(2,1)S(1)}) custom-call(bf16[128,8192]{1,0:T(8,128)(2,1)} %refs_0_.1), custom_call_target="tpu_custom_call" | custom-call | tf_op jit(solution)/shard_map/pack/pallas_call | solution.py:214
  2.1 0.0 copy-done.1
  2.1 4.0 %collective-permute-start.5 = (bf16[128,128]{1,0:T(8,128)(2,1)S(1)}, bf16[128,128]{1,0:T(8,128)(2,1)S(1)}, u32[]{:S(2)}, u32[]{:S(2)}) collective-permute-start(bf16[128,128]{1,0:T(8,128)(2,1)S(1)} %bitcast.11), channel_id=1, source_target_pairs={{0,24},{1,25},{2,26},{3,27},{4,28},{5,29},{6,30},{7,31},{8,16},{9,... | collective-permute-start | bytes 98312 | tf_op jit(solution)/shard_map/ppermute | solution.py:27
  6.1 0.5 %collective-permute-start.4 = (bf16[128,128]{1,0:T(8,128)(2,1)S(1)}, bf16[128,128]{1,0:T(8,128)(2,1)S(1)}, u32[]{:S(2)}, u32[]{:S(2)}) collective-permute-start(bf16[128,128]{1,0:T(8,128)(2,1)S(1)} %bitcast.12), channel_id=1, source_target_pairs={{0,16},{1,17},{2,18},{3,19},{4,20},{5,21},{6,22},{7,23},{8,24},{9,... | collective-permute-start | bytes 98312 | tf_op jit(solution)/shard_map/ppermute | solution.py:27
  6.6 0.1 collective-permute-start.3
  6.7 0.0 copy-done
  6.7 0.0 collective-permute-start.7
  6.7 1.9 %collective-permute-start = (bf16[128,1024]{1,0:T(8,128)(2,1)S(1)}, bf16[128,1024]{1,0:T(8,128)(2,1)S(1)}, u32[]{:S(2)}, u32[]{:S(2)}) collective-permute-start(bf16[128,1024]{1,0:T(8,128)(2,1)S(1)} %get-tuple-element.21), channel_id=1, source_target_pairs={{0,8},{1,9},{2,10},{3,11},{4,12},{5,13},{6,14},{7,15},{8,0},{9,1},... | collective-permute-start | bytes 786440 | tf_op jit(solution)/shard_map/ppermute | solution.py:27
  8.6 0.0 collective-permute-done.5.refs_7_
  8.6 1.5 %collective-permute-start.1 = (bf16[128,1024]{1,0:T(8,128)(2,1)S(1)}, bf16[128,1024]{1,0:T(8,128)(2,1)S(1)}, u32[]{:S(2)}, u32[]{:S(2)}) collective-permute-start(bf16[128,1024]{1,0:T(8,128)(2,1)S(1)} %get-tuple-element.22), channel_id=1, source_target_pairs={{0,16},{1,17},{2,18},{3,19},{4,20},{5,21},{6,22},{7,23},{8,24},{9,... | collective-permute-start | bytes 786440 | tf_op jit(solution)/shard_map/ppermute | solution.py:27
  10.1 0.0 collective-permute-done.4.refs_6_
  10.1 1.3 %collective-permute-start.2 = (bf16[128,1024]{1,0:T(8,128)(2,1)S(1)}, bf16[128,1024]{1,0:T(8,128)(2,1)S(1)}, u32[]{:S(2)}, u32[]{:S(2)}) collective-permute-start(bf16[128,1024]{1,0:T(8,128)(2,1)S(1)} %get-tuple-element.23), channel_id=1, source_target_pairs={{0,24},{1,25},{2,26},{3,27},{4,28},{5,29},{6,30},{7,31},{8,16},{9,... | collective-permute-start | bytes 786440 | tf_op jit(solution)/shard_map/ppermute | solution.py:27
  11.4 0.0 collective-permute-done.3.refs_5_
  11.4 1.6 %collective-permute-start.6 = (bf16[512,128]{1,0:T(8,128)(2,1)S(1)}, bf16[512,128]{1,0:T(8,128)(2,1)S(1)}, u32[]{:S(2)}, u32[]{:S(2)}) collective-permute-start(bf16[512,128]{1,0:T(8,128)(2,1)S(1)} %pad_maximum_fusion), channel_id=1, source_target_pairs={{0,1},{1,0},{2,3},{3,2},{4,5},{5,4},{6,7},{7,6},{8,9},{9,8},{10,11... | collective-permute-start | bytes 393224 | tf_op jit(solution)/shard_map/ppermute | solution.py:27
  13.1 3.4 %collective-permute-done.6.refs_8_ = bf16[512,128]{1,0:T(8,128)(2,1)S(1)} collective-permute-done((bf16[512,128]{1,0:T(8,128)(2,1)S(1)}, bf16[512,128]{1,0:T(8,128)(2,1)S(1)}, u32[]{:S(2)}, u32[]{:S(2)}) %collective-permute-start.6) | collective-permute-done | bytes 131104 | tf_op jit(solution)/shard_map/ppermute | solution.py:27
  16.4 0.0 collective-permute-done.7.twin_ref
  16.4 0.0 collective-permute-done.refs_1_
  16.5 5.3 %collective-permute-done.1.refs_2_ = bf16[128,1024]{1,0:T(8,128)(2,1)S(1)} collective-permute-done((bf16[128,1024]{1,0:T(8,128)(2,1)S(1)}, bf16[128,1024]{1,0:T(8,128)(2,1)S(1)}, u32[]{:S(2)}, u32[]{:S(2)}) %collective-permute-start.1) | collective-permute-done | bytes 262176 | tf_op jit(solution)/shard_map/ppermute | solution.py:27
  21.7 1.0 %collective-permute-done.2.refs_3_ = bf16[128,1024]{1,0:T(8,128)(2,1)S(1)} collective-permute-done((bf16[128,1024]{1,0:T(8,128)(2,1)S(1)}, bf16[128,1024]{1,0:T(8,128)(2,1)S(1)}, u32[]{:S(2)}, u32[]{:S(2)}) %collective-permute-start.2) | collective-permute-done | bytes 262176 | tf_op jit(solution)/shard_map/ppermute | solution.py:27
  22.7 0.5 %partial.1.own_ref = f32[1024,128]{1,0:T(8,128)S(1)} custom-call(bf16[128,1024]{1,0:T(8,128)(2,1)S(1)} %get-tuple-element.20.refs_0_, bf16[128,1024]{1,0:T(8,128)(2,1)S(1)} %collective-permute-done.refs_1_, bf16[128,1024]{1,0:T(8,128)(2,1)S(1)} %collective-permute-done.1.refs_2_, bf16[128,1024]{1,0:T(8,128)(2,1)S(1)} %collective-permute-done.2.refs_3_, ...), custom_call_target="tpu_custom_call" | custom-call | tf_op jit(solution)/shard_map/partial/pallas_call | solution.py:232
  23.2 0.1 collective-permute-start.8
  23.3 1.9 %collective-permute-done.8.other_ref = f32[1024,128]{1,0:T(8,128)S(1)} collective-permute-done((f32[1024,128]{1,0:T(8,128)S(1)}, f32[1024,128]{1,0:T(8,128)S(1)}, u32[]{:S(2)}, u32[]{:S(2)}) %collective-permute-start.8) | collective-permute-done | bytes 524320 | tf_op jit(solution)/shard_map/ppermute | solution.py:27
  25.2 0.5 %gradient.1 = (f32[512,128]{1,0:T(8,128)S(1)}, f32[512,128]{1,0:T(8,128)S(1)}, f32[72,128]{1,0:T(8,128)S(1)}) custom-call(f32[1024,128]{1,0:T(8,128)S(1)} %partial.1.own_ref, f32[1024,128]{1,0:T(8,128)S(1)} %collective-permute-done.8.other_ref, f32[512,128]{1,0:T(8,128)S(1)} %bitcast.10, f32[512,128]{1,0:T(8,128)S(1)} %collective-permute-done.7.twin_ref), custom_call_target="tpu_custom_call" | custom-call | tf_op jit(solution)/shard_map/gradient/pallas_call | solution.py:239
  25.7 1.5 %collective-permute-start.9 = (f32[72,128]{1,0:T(8,128)S(1)}, f32[72,128]{1,0:T(8,128)S(1)}, u32[]{:S(2)}, u32[]{:S(2)}) collective-permute-start(f32[72,128]{1,0:T(8,128)S(1)} %get-tuple-element.27), channel_id=1, source_target_pairs={{0,16},{1,17},{2,18},{3,19},{4,20},{5,21},{6,22},{7,23},{8,24},{9,... | collective-permute-start | bytes 110600 | tf_op jit(solution)/shard_map/ppermute | solution.py:27
  27.2 2.4 %collective-permute-done.9 = f32[72,128]{1,0:T(8,128)S(1)} collective-permute-done((f32[72,128]{1,0:T(8,128)S(1)}, f32[72,128]{1,0:T(8,128)S(1)}, u32[]{:S(2)}, u32[]{:S(2)}) %collective-permute-start.9) | collective-permute-done | bytes 36896 | tf_op jit(solution)/shard_map/ppermute | solution.py:27
  29.7 1.2 %collective-permute-start.10 = (f32[72,128]{1,0:T(8,128)S(1)}, f32[72,128]{1,0:T(8,128)S(1)}, u32[]{:S(2)}, u32[]{:S(2)}) collective-permute-start(f32[72,128]{1,0:T(8,128)S(1)} %add.6), channel_id=1, source_target_pairs={{0,8},{1,9},{2,10},{3,11},{4,12},{5,13},{6,14},{7,15},{8,0},{9,1},... | collective-permute-start | bytes 110600 | tf_op jit(solution)/shard_map/ppermute | solution.py:27
  30.9 2.7 %collective-permute-done.10 = f32[72,128]{1,0:T(8,128)S(1)} collective-permute-done((f32[72,128]{1,0:T(8,128)S(1)}, f32[72,128]{1,0:T(8,128)S(1)}, u32[]{:S(2)}, u32[]{:S(2)}) %collective-permute-start.10) | collective-permute-done | bytes 36896 | tf_op jit(solution)/shard_map/ppermute | solution.py:27
  33.6 1.6 %collective-permute-start.11 = (f32[72,128]{1,0:T(8,128)S(1)}, f32[72,128]{1,0:T(8,128)S(1)}, u32[]{:S(2)}, u32[]{:S(2)}) collective-permute-start(f32[72,128]{1,0:T(8,128)S(1)} %add.7.refs_0_), channel_id=1, source_target_pairs={{0,1},{1,0},{2,3},{3,2},{4,5},{5,4},{6,7},{7,6},{8,9},{9,8},{10,11... | collective-permute-start | bytes 110600 | tf_op jit(solution)/shard_map/ppermute | solution.py:27
  35.2 0.7 %copy.7 = f32[512,1,128]{2,1,0:T(1,128)} copy(f32[512,1,128]{2,1,0:T(1,128)S(1)} %bitcast.8) | data formatting | bytes 524288
  35.9 1.7 %collective-permute-done.11.refs_1_ = f32[72,128]{1,0:T(8,128)S(1)} collective-permute-done((f32[72,128]{1,0:T(8,128)S(1)}, f32[72,128]{1,0:T(8,128)S(1)}, u32[]{:S(2)}, u32[]{:S(2)}) %collective-permute-start.11) | collective-permute-done | bytes 36896 | tf_op jit(solution)/shard_map/ppermute | solution.py:27
  37.6 3.4 %newton.1 = f32[512,128]{1,0:T(8,128)} custom-call(f32[72,128]{1,0:T(8,128)S(1)} %add.7.refs_0_, f32[72,128]{1,0:T(8,128)S(1)} %collective-permute-done.11.refs_1_, f32[512,128]{1,0:T(8,128)S(1)} %get-tuple-element.28.refs_2_), custom_call_target="tpu_custom_call" | custom-call | tf_op jit(solution)/shard_map/newton/pallas_call | solution.py:269
  (3 shorter events, 0.0 us)
Async XLA Ops:
  0.6 1.4 %copy-start.1 = (bf16[128,1,128]{2,0,1:T(8,128)(2,1)S(1)}, bf16[128,1,128]{2,0,1:T(8,128)(2,1)}, u32[]{:S(2)}) copy-start(bf16[128,1,128]{2,0,1:T(8,128)(2,1)} %param.4) | copy-start | bytes 98308
  0.6 6.1 %copy-start = (f32[512,1,128]{2,1,0:T(1,128)S(1)}, f32[512,1,128]{2,1,0:T(1,128)}, u32[]{:S(2)}) copy-start(f32[512,1,128]{2,1,0:T(1,128)} %param.5) | copy-start | bytes 786436
  2.1 6.5 %collective-permute-start.5 = (bf16[128,128]{1,0:T(8,128)(2,1)S(1)}, bf16[128,128]{1,0:T(8,128)(2,1)S(1)}, u32[]{:S(2)}, u32[]{:S(2)}) collective-permute-start(bf16[128,128]{1,0:T(8,128)(2,1)S(1)} %bitcast.11), channel_id=1, source_target_pairs={{0,24},{1,25},{2,26},{3,27},{4,28},{5,29},{6,30},{7,31},{8,16},{9,... | collective-permute-start | bytes 98312 | tf_op jit(solution)/shard_map/ppermute | solution.py:27
  6.1 4.1 %collective-permute-start.4 = (bf16[128,128]{1,0:T(8,128)(2,1)S(1)}, bf16[128,128]{1,0:T(8,128)(2,1)S(1)}, u32[]{:S(2)}, u32[]{:S(2)}) collective-permute-start(bf16[128,128]{1,0:T(8,128)(2,1)S(1)} %bitcast.12), channel_id=1, source_target_pairs={{0,16},{1,17},{2,18},{3,19},{4,20},{5,21},{6,22},{7,23},{8,24},{9,... | collective-permute-start | bytes 98312 | tf_op jit(solution)/shard_map/ppermute | solution.py:27
  6.6 4.8 %collective-permute-start.3 = (bf16[128,128]{1,0:T(8,128)(2,1)S(1)}, bf16[128,128]{1,0:T(8,128)(2,1)S(1)}, u32[]{:S(2)}, u32[]{:S(2)}) collective-permute-start(bf16[128,128]{1,0:T(8,128)(2,1)S(1)} %bitcast.13), channel_id=1, source_target_pairs={{0,8},{1,9},{2,10},{3,11},{4,12},{5,13},{6,14},{7,15},{8,0},{9,1},... | collective-permute-start | bytes 98312 | tf_op jit(solution)/shard_map/ppermute | solution.py:27
  6.7 9.7 %collective-permute-start.7 = (f32[512,128]{1,0:T(8,128)S(1)}, f32[512,128]{1,0:T(8,128)S(1)}, u32[]{:S(2)}, u32[]{:S(2)}) collective-permute-start(f32[512,128]{1,0:T(8,128)S(1)} %bitcast.9), channel_id=1, source_target_pairs={{0,4},{1,5},{2,6},{3,7},{4,0},{5,1},{6,2},{7,3},{8,12},{9,13},{10,... | collective-permute-start | bytes 786440 | tf_op jit(solution)/shard_map/ppermute | solution.py:27
  6.7 9.7 %collective-permute-start = (bf16[128,1024]{1,0:T(8,128)(2,1)S(1)}, bf16[128,1024]{1,0:T(8,128)(2,1)S(1)}, u32[]{:S(2)}, u32[]{:S(2)}) collective-permute-start(bf16[128,1024]{1,0:T(8,128)(2,1)S(1)} %get-tuple-element.21), channel_id=1, source_target_pairs={{0,8},{1,9},{2,10},{3,11},{4,12},{5,13},{6,14},{7,15},{8,0},{9,1},... | collective-permute-start | bytes 786440 | tf_op jit(solution)/shard_map/ppermute | solution.py:27
  8.6 13.1 %collective-permute-start.1 = (bf16[128,1024]{1,0:T(8,128)(2,1)S(1)}, bf16[128,1024]{1,0:T(8,128)(2,1)S(1)}, u32[]{:S(2)}, u32[]{:S(2)}) collective-permute-start(bf16[128,1024]{1,0:T(8,128)(2,1)S(1)} %get-tuple-element.22), channel_id=1, source_target_pairs={{0,16},{1,17},{2,18},{3,19},{4,20},{5,21},{6,22},{7,23},{8,24},{9,... | collective-permute-start | bytes 786440 | tf_op jit(solution)/shard_map/ppermute | solution.py:27
  10.1 12.5 %collective-permute-start.2 = (bf16[128,1024]{1,0:T(8,128)(2,1)S(1)}, bf16[128,1024]{1,0:T(8,128)(2,1)S(1)}, u32[]{:S(2)}, u32[]{:S(2)}) collective-permute-start(bf16[128,1024]{1,0:T(8,128)(2,1)S(1)} %get-tuple-element.23), channel_id=1, source_target_pairs={{0,24},{1,25},{2,26},{3,27},{4,28},{5,29},{6,30},{7,31},{8,16},{9,... | collective-permute-start | bytes 786440 | tf_op jit(solution)/shard_map/ppermute | solution.py:27
  11.4 5.0 %collective-permute-start.6 = (bf16[512,128]{1,0:T(8,128)(2,1)S(1)}, bf16[512,128]{1,0:T(8,128)(2,1)S(1)}, u32[]{:S(2)}, u32[]{:S(2)}) collective-permute-start(bf16[512,128]{1,0:T(8,128)(2,1)S(1)} %pad_maximum_fusion), channel_id=1, source_target_pairs={{0,1},{1,0},{2,3},{3,2},{4,5},{5,4},{6,7},{7,6},{8,9},{9,8},{10,11... | collective-permute-start | bytes 393224 | tf_op jit(solution)/shard_map/ppermute | solution.py:27
  23.2 2.0 %collective-permute-start.8 = (f32[1024,128]{1,0:T(8,128)S(1)}, f32[1024,128]{1,0:T(8,128)S(1)}, u32[]{:S(2)}, u32[]{:S(2)}) collective-permute-start(f32[1024,128]{1,0:T(8,128)S(1)} %partial.1.own_ref), channel_id=1, source_target_pairs={{0,4},{1,5},{2,6},{3,7},{4,0},{5,1},{6,2},{7,3},{8,12},{9,13},{10,... | collective-permute-start | bytes 1572872 | tf_op jit(solution)/shard_map/ppermute | solution.py:27
  25.7 4.0 %collective-permute-start.9 = (f32[72,128]{1,0:T(8,128)S(1)}, f32[72,128]{1,0:T(8,128)S(1)}, u32[]{:S(2)}, u32[]{:S(2)}) collective-permute-start(f32[72,128]{1,0:T(8,128)S(1)} %get-tuple-element.27), channel_id=1, source_target_pairs={{0,16},{1,17},{2,18},{3,19},{4,20},{5,21},{6,22},{7,23},{8,24},{9,... | collective-permute-start | bytes 110600 | tf_op jit(solution)/shard_map/ppermute | solution.py:27
  29.7 4.0 %collective-permute-start.10 = (f32[72,128]{1,0:T(8,128)S(1)}, f32[72,128]{1,0:T(8,128)S(1)}, u32[]{:S(2)}, u32[]{:S(2)}) collective-permute-start(f32[72,128]{1,0:T(8,128)S(1)} %add.6), channel_id=1, source_target_pairs={{0,8},{1,9},{2,10},{3,11},{4,12},{5,13},{6,14},{7,15},{8,0},{9,1},... | collective-permute-start | bytes 110600 | tf_op jit(solution)/shard_map/ppermute | solution.py:27
  33.6 4.0 %collective-permute-start.11 = (f32[72,128]{1,0:T(8,128)S(1)}, f32[72,128]{1,0:T(8,128)S(1)}, u32[]{:S(2)}, u32[]{:S(2)}) collective-permute-start(f32[72,128]{1,0:T(8,128)S(1)} %add.7.refs_0_), channel_id=1, source_target_pairs={{0,1},{1,0},{2,3},{3,2},{4,5},{5,4},{6,7},{7,6},{8,9},{9,8},{10,11... | collective-permute-start | bytes 110600 | tf_op jit(solution)/shard_map/ppermute | solution.py:27

commit v3 on v2

--- a/solution.py
+++ b/solution.py
@@ -110,8 +110,7 @@
 
 
 def partial_kernel(n_pieces, *refs):
-    features, keys = refs[:n_pieces], refs[n_pieces : 2 * n_pieces]
-    partner_ref, grads_ref = refs[2 * n_pieces :]
+    features, keys, partner_ref, grads_ref = refs[:n_pieces], refs[n_pieces:-2], refs[-2], refs[-1]
     head_size = grads_ref.shape[1]
     own = jnp.concatenate([key[...] for key in keys], axis=0)
     keys = jnp.concatenate([own, partner_ref[...]], axis=1)
@@ -205,12 +204,16 @@
     tokens, head_size = own_part.shape
     rows_half = moment.shape[0]
     bits = [1 << b for b in reversed(range(n_fsdp.bit_length() - 1))]
-    direct = n_fsdp == 1 << len(bits) and n_fsdp <= 16 and rows_half % 128 == 0 and n_tp & (n_tp - 1) == 0
+    direct = n_fsdp == 1 << len(bits) and n_fsdp <= 8 and rows_half % 128 == 0 and n_tp & (n_tp - 1) == 0
     block = pltpu.VMEM((rows_half, head_size), jnp.float32)
     small = pltpu.VMEM((head_size // 2 + 8, head_size), jnp.float32)
     if direct:
         n_chip = n_fsdp // 2
+        gathered, stages = own_part, [own_part]
         packed = pltpu.VMEM((tokens, 2 * rows_half), features.dtype)
+        for bit in bits[-2::-1]:
+            stages.append(swapped(gathered, bit, 0))
+            gathered = jnp.concatenate([gathered, stages[-1]], axis=0)
         pieces = pl.pallas_call(
             lambda *refs: pack_kernel(rows_half, *refs),
             out_shape=(packed,) * n_chip,
@@ -219,23 +222,19 @@
             scratch_shapes=[pltpu.SemaphoreType.DMA((2 * n_chip,))],
             name="pack",
         )(features)
-        pieces, own_part = lax.optimization_barrier((pieces, own_part))
         pieces = list(pieces)
         for d in range(1, n_chip):
             pieces[d] = swapped(pieces[d], 2 * d, 0)
-        keys = [own_part]
-        for d in range(1, n_chip):
-            keys.append(swapped(own_part, 2 * d, 0))
-        partner_keys = swapped(jnp.concatenate(keys, axis=0), 0, 1)
+        partner_keys = swapped(gathered, 0, 1)
         twin = swapped(moment, 1, 0)
         partner_keys, twin = lax.optimization_barrier((partner_keys, twin))
         grads = pl.pallas_call(
             lambda *refs: partial_kernel(n_chip, *refs),
             out_shape=pltpu.VMEM((2 * rows_half, head_size), jnp.float32),
-            in_specs=whole(2 * n_chip + 1),
+            in_specs=whole(n_chip + len(stages) + 1),
             out_specs=whole(1)[0],
             name="partial",
-        )(*on_chip(*pieces, *keys, partner_keys))
+        )(*on_chip(*pieces, *stages, partner_keys))
         fresh, blend, gram = pl.pallas_call(
             joined_kernel,
             out_shape=(block, block, small),
@@ -243,8 +242,11 @@
             out_specs=tuple(whole(3)),
             name="gradient",
         )(*on_chip(grads, swapped(grads, 1, 0), moment, twin))
-        for bit in bits[:-1]:
-            gram = gram + swapped(gram, bit, 0)
+        others = []
+        for d in reversed(range(1, n_chip)):
+            others.append(swapped(gram, 2 * d, 0))
+        for other in others:
+            gram = gram + other
         grams = [gram, swapped(gram, 0, 1)]
     else:
         shard = lax.psum_scatter(

time: 41.1 us -> 42.8 us (1.041)
  waiting for transfers between devices: 18.4 us -> 19.2 us
  other arithmetic: 0.02 us -> 0.78 us
    concatenate x1 -> x2, other arithmetic: 0.01 us -> 0.77 us  [ordered(): gathered = jnp.concatenate([gathered, stages[-1]], axis=0)]
    ppermute x12, waiting for transfers between devices: 18.4 us -> 19.2 us  [swapped(): lax.ppermute(block, ('fsdp', 'tp'), [(i, i ^ mask) for i in range(count)])]
  transfers between devices with their start and end apart: 12 -> 12, of which waited for: 7 -> 9; matrix products, arithmetic and copies ran while one was open for 2% -> 2% of each run, Pallas kernels for 0% -> 3%
where the time goes in v3:
time: 42.8 us; the launch traced here: 42.6 us
  waiting for transfers between devices  19.2 us (45%)
  starting transfers between devices  15.5 us (36%)
  Pallas kernels  5.82 us (14%)
  other arithmetic  0.78 us (2%)
  local copies, waits for them, and re-layouts  0.71 us (2%)
  between operations  0.68 us (2%)
    ppermute x12, waiting for transfers between devices, swapped(): lax.ppermute(block, ('fsdp', 'tp'), [(i, i ^ mask) for i in range(count)])  19.2 us
    ppermute x12, starting transfers between devices, swapped(): lax.ppermute(block, ('fsdp', 'tp'), [(i, i ^ mask) for i in range(count)])  15.5 us
    pallas_call x1, Pallas kernels, ordered(): pl.pallas_call(lambda *refs: newton_kernel(scale, len(grams), *refs), out...  3.38 us
    pallas_call x1, Pallas kernels, ordered(): pl.pallas_call(lambda *refs: pack_kernel(rows_half, *refs), out_shape=(pa...  1.39 us
  transfers between devices with their start and end apart: 12, of which 9 were waited for; matrix products, arithmetic and copies ran while one was open for 2% of the time, Pallas kernels for 3%

profile of v3, /device:TPU:0, one launch (start us, length us, event | category | flops | bytes accessed | tf_op | source)
XLA Modules:
  0.0 42.6 jit_solution(4118036524455936262)
XLA Ops:
  0.6 0.0 copy-start
  0.6 3.0 %collective-permute-start.3 = (bf16[128,128]{1,0:T(8,128)(2,1)}, bf16[128,128]{1,0:T(8,128)(2,1)S(1)}, u32[]{:S(2)}, u32[]{:S(2)}) collective-permute-start(bf16[128,128]{1,0:T(8,128)(2,1)} %bitcast.9), channel_id=1, source_target_pairs={{0,8},{1,9},{2,10},{3,11},{4,12},{5,13},{6,14},{7,15},{8,0},{9,1},... | collective-permute-start | bytes 98312 | tf_op jit(solution)/shard_map/ppermute | solution.py:27
  3.7 2.1 %collective-permute-done.3.refs_5_ = bf16[128,128]{1,0:T(8,128)(2,1)S(1)} collective-permute-done((bf16[128,128]{1,0:T(8,128)(2,1)}, bf16[128,128]{1,0:T(8,128)(2,1)S(1)}, u32[]{:S(2)}, u32[]{:S(2)}) %collective-permute-start.3) | collective-permute-done | bytes 32800 | tf_op jit(solution)/shard_map/ppermute | solution.py:27
  5.8 0.8 %pad_maximum_fusion.1 = bf16[256,128]{1,0:T(8,128)(2,1)S(1)} fusion(bf16[128,128]{1,0:T(8,128)(2,1)S(1)} %collective-permute-done.3.refs_5_, bf16[128,128]{1,0:T(8,128)(2,1)} %bitcast.10), kind=kLoop, calls=%fused_computation.1 | loop fusion | flops 131072 | bytes 131072 | tf_op jit(solution)/shard_map/concatenate | solution.py:216
  6.5 2.0 %collective-permute-start.4 = (bf16[256,128]{1,0:T(8,128)(2,1)S(1)}, bf16[256,128]{1,0:T(8,128)(2,1)S(1)}, u32[]{:S(2)}, u32[]{:S(2)}) collective-permute-start(bf16[256,128]{1,0:T(8,128)(2,1)S(1)} %pad_maximum_fusion.1), channel_id=1, source_target_pairs={{0,16},{1,17},{2,18},{3,19},{4,20},{5,21},{6,22},{7,23},{8,24},{9,... | collective-permute-start | bytes 196616 | tf_op jit(solution)/shard_map/ppermute | solution.py:27
  8.6 0.0 copy-start.1
  8.6 0.0 collective-permute-start.6
  8.6 1.4 %pack.1 = (bf16[128,1024]{1,0:T(8,128)(2,1)S(1)}, bf16[128,1024]{1,0:T(8,128)(2,1)S(1)}, bf16[128,1024]{1,0:T(8,128)(2,1)S(1)}, bf16[128,1024]{1,0:T(8,128)(2,1)S(1)}) custom-call(bf16[128,8192]{1,0:T(8,128)(2,1)} %refs_0_.1), custom_call_target="tpu_custom_call" | custom-call | tf_op jit(solution)/shard_map/pack/pallas_call | solution.py:217
  10.0 1.6 %collective-permute-start = (bf16[128,1024]{1,0:T(8,128)(2,1)S(1)}, bf16[128,1024]{1,0:T(8,128)(2,1)S(1)}, u32[]{:S(2)}, u32[]{:S(2)}) collective-permute-start(bf16[128,1024]{1,0:T(8,128)(2,1)S(1)} %get-tuple-element.12), channel_id=1, source_target_pairs={{0,8},{1,9},{2,10},{3,11},{4,12},{5,13},{6,14},{7,15},{8,0},{9,1},... | collective-permute-start | bytes 786440 | tf_op jit(solution)/shard_map/ppermute | solution.py:27
  11.6 0.5 %collective-permute-start.1 = (bf16[128,1024]{1,0:T(8,128)(2,1)S(1)}, bf16[128,1024]{1,0:T(8,128)(2,1)S(1)}, u32[]{:S(2)}, u32[]{:S(2)}) collective-permute-start(bf16[128,1024]{1,0:T(8,128)(2,1)S(1)} %get-tuple-element.13), channel_id=1, source_target_pairs={{0,16},{1,17},{2,18},{3,19},{4,20},{5,21},{6,22},{7,23},{8,24},{9,... | collective-permute-start | bytes 786440 | tf_op jit(solution)/shard_map/ppermute | solution.py:27
  12.1 1.5 %collective-permute-start.2 = (bf16[128,1024]{1,0:T(8,128)(2,1)S(1)}, bf16[128,1024]{1,0:T(8,128)(2,1)S(1)}, u32[]{:S(2)}, u32[]{:S(2)}) collective-permute-start(bf16[128,1024]{1,0:T(8,128)(2,1)S(1)} %get-tuple-element.14), channel_id=1, source_target_pairs={{0,24},{1,25},{2,26},{3,27},{4,28},{5,29},{6,30},{7,31},{8,16},{9,... | collective-permute-start | bytes 786440 | tf_op jit(solution)/shard_map/ppermute | solution.py:27
  13.5 0.0 collective-permute-done.4.refs_6_
  13.6 0.0 copy-done
  13.6 1.6 %collective-permute-start.5 = (bf16[512,128]{1,0:T(8,128)(2,1)S(1)}, bf16[512,128]{1,0:T(8,128)(2,1)S(1)}, u32[]{:S(2)}, u32[]{:S(2)}) collective-permute-start(bf16[512,128]{1,0:T(8,128)(2,1)S(1)} %pad_maximum_fusion), channel_id=1, source_target_pairs={{0,1},{1,0},{2,3},{3,2},{4,5},{5,4},{6,7},{7,6},{8,9},{9,8},{10,11... | collective-permute-start | bytes 393224 | tf_op jit(solution)/shard_map/ppermute | solution.py:27
  15.2 3.5 %collective-permute-done.5.refs_7_ = bf16[512,128]{1,0:T(8,128)(2,1)S(1)} collective-permute-done((bf16[512,128]{1,0:T(8,128)(2,1)S(1)}, bf16[512,128]{1,0:T(8,128)(2,1)S(1)}, u32[]{:S(2)}, u32[]{:S(2)}) %collective-permute-start.5) | collective-permute-done | bytes 131104 | tf_op jit(solution)/shard_map/ppermute | solution.py:27
  18.7 0.0 collective-permute-done.6.twin_ref
  18.7 0.6 %collective-permute-done.refs_1_ = bf16[128,1024]{1,0:T(8,128)(2,1)S(1)} collective-permute-done((bf16[128,1024]{1,0:T(8,128)(2,1)S(1)}, bf16[128,1024]{1,0:T(8,128)(2,1)S(1)}, u32[]{:S(2)}, u32[]{:S(2)}) %collective-permute-start) | collective-permute-done | bytes 262176 | tf_op jit(solution)/shard_map/ppermute | solution.py:27
  19.2 6.3 %collective-permute-done.1.refs_2_ = bf16[128,1024]{1,0:T(8,128)(2,1)S(1)} collective-permute-done((bf16[128,1024]{1,0:T(8,128)(2,1)S(1)}, bf16[128,1024]{1,0:T(8,128)(2,1)S(1)}, u32[]{:S(2)}, u32[]{:S(2)}) %collective-permute-start.1) | collective-permute-done | bytes 262176 | tf_op jit(solution)/shard_map/ppermute | solution.py:27
  25.6 0.0 collective-permute-done.2.refs_3_
  25.6 0.5 %partial.1.own_ref = f32[1024,128]{1,0:T(8,128)S(1)} custom-call(bf16[128,1024]{1,0:T(8,128)(2,1)S(1)} %get-tuple-element.11.refs_0_, bf16[128,1024]{1,0:T(8,128)(2,1)S(1)} %collective-permute-done.refs_1_, bf16[128,1024]{1,0:T(8,128)(2,1)S(1)} %collective-permute-done.1.refs_2_, bf16[128,1024]{1,0:T(8,128)(2,1)S(1)} %collective-permute-done.2.refs_3_, ...), custom_call_target="tpu_custom_call" | custom-call | tf_op jit(solution)/shard_map/partial/pallas_call | solution.py:231
  26.1 0.1 collective-permute-start.7
  26.2 1.9 %collective-permute-done.7.other_ref = f32[1024,128]{1,0:T(8,128)S(1)} collective-permute-done((f32[1024,128]{1,0:T(8,128)S(1)}, f32[1024,128]{1,0:T(8,128)S(1)}, u32[]{:S(2)}, u32[]{:S(2)}) %collective-permute-start.7) | collective-permute-done | bytes 524320 | tf_op jit(solution)/shard_map/ppermute | solution.py:27
  28.1 0.0 copy-done.1
  28.1 0.5 %gradient.1 = (f32[512,128]{1,0:T(8,128)S(1)}, f32[512,128]{1,0:T(8,128)S(1)}, f32[72,128]{1,0:T(8,128)S(1)}) custom-call(f32[1024,128]{1,0:T(8,128)S(1)} %partial.1.own_ref, f32[1024,128]{1,0:T(8,128)S(1)} %collective-permute-done.7.other_ref, f32[512,128]{1,0:T(8,128)S(1)} %bitcast.14, f32[512,128]{1,0:T(8,128)S(1)} %collective-permute-done.6.twin_ref), custom_call_target="tpu_custom_call" | custom-call | tf_op jit(solution)/shard_map/gradient/pallas_call | solution.py:238
  28.6 0.5 %collective-permute-start.10 = (f32[72,128]{1,0:T(8,128)S(1)}, f32[72,128]{1,0:T(8,128)S(1)}, u32[]{:S(2)}, u32[]{:S(2)}) collective-permute-start(f32[72,128]{1,0:T(8,128)S(1)} %get-tuple-element.17), channel_id=1, source_target_pairs={{0,8},{1,9},{2,10},{3,11},{4,12},{5,13},{6,14},{7,15},{8,0},{9,1},... | collective-permute-start | bytes 110600 | tf_op jit(solution)/shard_map/ppermute | solution.py:27
  29.2 1.2 %collective-permute-start.9 = (f32[72,128]{1,0:T(8,128)S(1)}, f32[72,128]{1,0:T(8,128)S(1)}, u32[]{:S(2)}, u32[]{:S(2)}) collective-permute-start(f32[72,128]{1,0:T(8,128)S(1)} %get-tuple-element.17), channel_id=1, source_target_pairs={{0,16},{1,17},{2,18},{3,19},{4,20},{5,21},{6,22},{7,23},{8,24},{9,... | collective-permute-start | bytes 110600 | tf_op jit(solution)/shard_map/ppermute | solution.py:27
  30.4 1.7 %collective-permute-start.8 = (f32[72,128]{1,0:T(8,128)S(1)}, f32[72,128]{1,0:T(8,128)S(1)}, u32[]{:S(2)}, u32[]{:S(2)}) collective-permute-start(f32[72,128]{1,0:T(8,128)S(1)} %get-tuple-element.17), channel_id=1, source_target_pairs={{0,24},{1,25},{2,26},{3,27},{4,28},{5,29},{6,30},{7,31},{8,16},{9,... | collective-permute-start | bytes 110600 | tf_op jit(solution)/shard_map/ppermute | solution.py:27
  32.1 0.5 %collective-permute-done.10 = f32[72,128]{1,0:T(8,128)S(1)} collective-permute-done((f32[72,128]{1,0:T(8,128)S(1)}, f32[72,128]{1,0:T(8,128)S(1)}, u32[]{:S(2)}, u32[]{:S(2)}) %collective-permute-start.10) | collective-permute-done | bytes 36896 | tf_op jit(solution)/shard_map/ppermute | solution.py:27
  32.6 0.5 %collective-permute-done.9 = f32[72,128]{1,0:T(8,128)S(1)} collective-permute-done((f32[72,128]{1,0:T(8,128)S(1)}, f32[72,128]{1,0:T(8,128)S(1)}, u32[]{:S(2)}, u32[]{:S(2)}) %collective-permute-start.9) | collective-permute-done | bytes 36896 | tf_op jit(solution)/shard_map/ppermute | solution.py:27
  33.1 2.1 %collective-permute-done.8 = f32[72,128]{1,0:T(8,128)S(1)} collective-permute-done((f32[72,128]{1,0:T(8,128)S(1)}, f32[72,128]{1,0:T(8,128)S(1)}, u32[]{:S(2)}, u32[]{:S(2)}) %collective-permute-start.8) | collective-permute-done | bytes 36896 | tf_op jit(solution)/shard_map/ppermute | solution.py:27
  35.2 1.6 %collective-permute-start.11 = (f32[72,128]{1,0:T(8,128)S(1)}, f32[72,128]{1,0:T(8,128)S(1)}, u32[]{:S(2)}, u32[]{:S(2)}) collective-permute-start(f32[72,128]{1,0:T(8,128)S(1)} %add_add_fusion.refs_0_), channel_id=1, source_target_pairs={{0,1},{1,0},{2,3},{3,2},{4,5},{5,4},{6,7},{7,6},{8,9},{9,8},{10,11... | collective-permute-start | bytes 110600 | tf_op jit(solution)/shard_map/ppermute | solution.py:27
  36.9 0.7 %copy.7 = f32[512,1,128]{2,1,0:T(1,128)} copy(f32[512,1,128]{2,1,0:T(1,128)S(1)} %bitcast.8) | data formatting | bytes 524288
  37.6 1.7 %collective-permute-done.11.refs_1_ = f32[72,128]{1,0:T(8,128)S(1)} collective-permute-done((f32[72,128]{1,0:T(8,128)S(1)}, f32[72,128]{1,0:T(8,128)S(1)}, u32[]{:S(2)}, u32[]{:S(2)}) %collective-permute-start.11) | collective-permute-done | bytes 36896 | tf_op jit(solution)/shard_map/ppermute | solution.py:27
  39.3 3.4 %newton.1 = f32[512,128]{1,0:T(8,128)} custom-call(f32[72,128]{1,0:T(8,128)S(1)} %add_add_fusion.refs_0_, f32[72,128]{1,0:T(8,128)S(1)} %collective-permute-done.11.refs_1_, f32[512,128]{1,0:T(8,128)S(1)} %get-tuple-element.18.refs_2_), custom_call_target="tpu_custom_call" | custom-call | tf_op jit(solution)/shard_map/newton/pallas_call | solution.py:271
  (2 shorter events, 0.0 us)
Async XLA Ops:
  0.6 12.9 %copy-start = (bf16[128,1,128]{2,0,1:T(8,128)(2,1)S(1)}, bf16[128,1,128]{2,0,1:T(8,128)(2,1)}, u32[]{:S(2)}) copy-start(bf16[128,1,128]{2,0,1:T(8,128)(2,1)} %param.4) | copy-start | bytes 98308
  0.6 5.1 %collective-permute-start.3 = (bf16[128,128]{1,0:T(8,128)(2,1)}, bf16[128,128]{1,0:T(8,128)(2,1)S(1)}, u32[]{:S(2)}, u32[]{:S(2)}) collective-permute-start(bf16[128,128]{1,0:T(8,128)(2,1)} %bitcast.9), channel_id=1, source_target_pairs={{0,8},{1,9},{2,10},{3,11},{4,12},{5,13},{6,14},{7,15},{8,0},{9,1},... | collective-permute-start | bytes 98312 | tf_op jit(solution)/shard_map/ppermute | solution.py:27
  6.5 7.0 %collective-permute-start.4 = (bf16[256,128]{1,0:T(8,128)(2,1)S(1)}, bf16[256,128]{1,0:T(8,128)(2,1)S(1)}, u32[]{:S(2)}, u32[]{:S(2)}) collective-permute-start(bf16[256,128]{1,0:T(8,128)(2,1)S(1)} %pad_maximum_fusion.1), channel_id=1, source_target_pairs={{0,16},{1,17},{2,18},{3,19},{4,20},{5,21},{6,22},{7,23},{8,24},{9,... | collective-permute-start | bytes 196616 | tf_op jit(solution)/shard_map/ppermute | solution.py:27
  8.6 19.5 %copy-start.1 = (f32[512,1,128]{2,1,0:T(1,128)S(1)}, f32[512,1,128]{2,1,0:T(1,128)}, u32[]{:S(2)}) copy-start(f32[512,1,128]{2,1,0:T(1,128)} %param.5) | copy-start | bytes 786436
  8.6 10.1 %collective-permute-start.6 = (f32[512,128]{1,0:T(8,128)}, f32[512,128]{1,0:T(8,128)S(1)}, u32[]{:S(2)}, u32[]{:S(2)}) collective-permute-start(f32[512,128]{1,0:T(8,128)} %bitcast.13), channel_id=1, source_target_pairs={{0,4},{1,5},{2,6},{3,7},{4,0},{5,1},{6,2},{7,3},{8,12},{9,13},{10,... | collective-permute-start | bytes 786440 | tf_op jit(solution)/shard_map/ppermute | solution.py:27
  10.0 9.2 %collective-permute-start = (bf16[128,1024]{1,0:T(8,128)(2,1)S(1)}, bf16[128,1024]{1,0:T(8,128)(2,1)S(1)}, u32[]{:S(2)}, u32[]{:S(2)}) collective-permute-start(bf16[128,1024]{1,0:T(8,128)(2,1)S(1)} %get-tuple-element.12), channel_id=1, source_target_pairs={{0,8},{1,9},{2,10},{3,11},{4,12},{5,13},{6,14},{7,15},{8,0},{9,1},... | collective-permute-start | bytes 786440 | tf_op jit(solution)/shard_map/ppermute | solution.py:27
  11.6 14.0 %collective-permute-start.1 = (bf16[128,1024]{1,0:T(8,128)(2,1)S(1)}, bf16[128,1024]{1,0:T(8,128)(2,1)S(1)}, u32[]{:S(2)}, u32[]{:S(2)}) collective-permute-start(bf16[128,1024]{1,0:T(8,128)(2,1)S(1)} %get-tuple-element.13), channel_id=1, source_target_pairs={{0,16},{1,17},{2,18},{3,19},{4,20},{5,21},{6,22},{7,23},{8,24},{9,... | collective-permute-start | bytes 786440 | tf_op jit(solution)/shard_map/ppermute | solution.py:27
  12.1 13.5 %collective-permute-start.2 = (bf16[128,1024]{1,0:T(8,128)(2,1)S(1)}, bf16[128,1024]{1,0:T(8,128)(2,1)S(1)}, u32[]{:S(2)}, u32[]{:S(2)}) collective-permute-start(bf16[128,1024]{1,0:T(8,128)(2,1)S(1)} %get-tuple-element.14), channel_id=1, source_target_pairs={{0,24},{1,25},{2,26},{3,27},{4,28},{5,29},{6,30},{7,31},{8,16},{9,... | collective-permute-start | bytes 786440 | tf_op jit(solution)/shard_map/ppermute | solution.py:27
  13.6 5.1 %collective-permute-start.5 = (bf16[512,128]{1,0:T(8,128)(2,1)S(1)}, bf16[512,128]{1,0:T(8,128)(2,1)S(1)}, u32[]{:S(2)}, u32[]{:S(2)}) collective-permute-start(bf16[512,128]{1,0:T(8,128)(2,1)S(1)} %pad_maximum_fusion), channel_id=1, source_target_pairs={{0,1},{1,0},{2,3},{3,2},{4,5},{5,4},{6,7},{7,6},{8,9},{9,8},{10,11... | collective-permute-start | bytes 393224 | tf_op jit(solution)/shard_map/ppermute | solution.py:27
  26.1 2.0 %collective-permute-start.7 = (f32[1024,128]{1,0:T(8,128)S(1)}, f32[1024,128]{1,0:T(8,128)S(1)}, u32[]{:S(2)}, u32[]{:S(2)}) collective-permute-start(f32[1024,128]{1,0:T(8,128)S(1)} %partial.1.own_ref), channel_id=1, source_target_pairs={{0,4},{1,5},{2,6},{3,7},{4,0},{5,1},{6,2},{7,3},{8,12},{9,13},{10,... | collective-permute-start | bytes 1572872 | tf_op jit(solution)/shard_map/ppermute | solution.py:27
  28.6 4.0 %collective-permute-start.10 = (f32[72,128]{1,0:T(8,128)S(1)}, f32[72,128]{1,0:T(8,128)S(1)}, u32[]{:S(2)}, u32[]{:S(2)}) collective-permute-start(f32[72,128]{1,0:T(8,128)S(1)} %get-tuple-element.17), channel_id=1, source_target_pairs={{0,8},{1,9},{2,10},{3,11},{4,12},{5,13},{6,14},{7,15},{8,0},{9,1},... | collective-permute-start | bytes 110600 | tf_op jit(solution)/shard_map/ppermute | solution.py:27
  29.2 4.0 %collective-permute-start.9 = (f32[72,128]{1,0:T(8,128)S(1)}, f32[72,128]{1,0:T(8,128)S(1)}, u32[]{:S(2)}, u32[]{:S(2)}) collective-permute-start(f32[72,128]{1,0:T(8,128)S(1)} %get-tuple-element.17), channel_id=1, source_target_pairs={{0,16},{1,17},{2,18},{3,19},{4,20},{5,21},{6,22},{7,23},{8,24},{9,... | collective-permute-start | bytes 110600 | tf_op jit(solution)/shard_map/ppermute | solution.py:27
  30.4 4.9 %collective-permute-start.8 = (f32[72,128]{1,0:T(8,128)S(1)}, f32[72,128]{1,0:T(8,128)S(1)}, u32[]{:S(2)}, u32[]{:S(2)}) collective-permute-start(f32[72,128]{1,0:T(8,128)S(1)} %get-tuple-element.17), channel_id=1, source_target_pairs={{0,24},{1,25},{2,26},{3,27},{4,28},{5,29},{6,30},{7,31},{8,16},{9,... | collective-permute-start | bytes 110600 | tf_op jit(solution)/shard_map/ppermute | solution.py:27
  35.2 4.0 %collective-permute-start.11 = (f32[72,128]{1,0:T(8,128)S(1)}, f32[72,128]{1,0:T(8,128)S(1)}, u32[]{:S(2)}, u32[]{:S(2)}) collective-permute-start(f32[72,128]{1,0:T(8,128)S(1)} %add_add_fusion.refs_0_), channel_id=1, source_target_pairs={{0,1},{1,0},{2,3},{3,2},{4,5},{5,4},{6,7},{7,6},{8,9},{9,8},{10,11... | collective-permute-start | bytes 110600 | tf_op jit(solution)/shard_map/ppermute | solution.py:27

commit v4 on v3

--- a/solution.py
+++ b/solution.py
@@ -20,11 +20,17 @@
 contract = (((0,), (0,)), ((), ()))
 
 
-def swapped(block, fsdp_bits, tp_bits):
+def swapped(block, fsdp_bits, tp_bits, odd_bits=None):
     n_tp = lax.axis_size("tp")
     count = lax.axis_size("fsdp") * n_tp
-    mask = fsdp_bits * n_tp + tp_bits
-    return lax.ppermute(block, ("fsdp", "tp"), [(i, i ^ mask) for i in range(count)])
+    choices = (fsdp_bits, fsdp_bits if odd_bits is None else odd_bits)
+    masks = [choices[i // n_tp % 2] * n_tp + tp_bits for i in range(count)]
+    return lax.ppermute(block, ("fsdp", "tp"), [(i, i ^ mask) for i, mask in enumerate(masks)])
+
+
+def turned(distance, n_chip):
+    width = n_chip.bit_length() - 1
+    return sum((distance >> i & 1) << (width - 1 - i) for i in range(width))
 
 
 def halves(value):
@@ -86,23 +92,25 @@
     return fresh, grads + retain * fresh
 
 
-def pack_kernel(width, features_ref, *refs):
+def far(distance):
+    return distance & (distance - 1) != 0
+
+
+def pack_kernel(width, features_ref, keys_ref, *refs):
     outs, sems = refs[:-1], refs[-1]
     index = lax.axis_index("fsdp")
     parity = lax.axis_index("tp") % 2
     chip, core = index // 2, index % 2
     copies = []
     for i, out in enumerate(outs):
+        distance = jnp.where(core == 0, i, turned(i, len(outs)))
         for j in range(2):
-            block = (chip ^ i) * 2 + (core ^ j)
+            block = (chip ^ distance) * 2 + (core ^ j)
             start = pl.multiple_of((block * 2 + parity) * width, width)
-            copies.append(
-                pltpu.make_async_copy(
-                    features_ref.at[:, pl.ds(start, width)],
-                    out.at[:, pl.ds(j * width, width)],
-                    sems.at[2 * i + j],
-                )
-            )
+            copies.append((features_ref.at[:, pl.ds(start, width)], out.at[:, pl.ds(j * width, width)]))
+        if out.shape[1] > 2 * width:
+            copies.append((keys_ref, out.at[:, pl.ds(2 * width, keys_ref.shape[1])]))
+    copies = [pltpu.make_async_copy(*ends, sems.at[i]) for i, ends in enumerate(copies)]
     for copy in copies:
         copy.start()
     for copy in copies:
@@ -110,11 +118,12 @@
 
 
 def partial_kernel(n_pieces, *refs):
-    features, keys, partner_ref, grads_ref = refs[:n_pieces], refs[n_pieces:-2], refs[-2], refs[-1]
-    head_size = grads_ref.shape[1]
-    own = jnp.concatenate([key[...] for key in keys], axis=0)
-    keys = jnp.concatenate([own, partner_ref[...]], axis=1)
-    features = jnp.concatenate([piece[...] for piece in features], axis=0)
+    features, keys, grads_ref = refs[:n_pieces], list(refs[n_pieces:-1]), refs[-1]
+    rows, head_size = grads_ref.shape
+    own = [keys.pop(0)[...] if not i or far(i) else piece[:, rows:] for i, piece in enumerate(features)]
+    partner = [ref[...] for ref in keys]
+    keys = jnp.concatenate([jnp.concatenate(own, axis=0), jnp.concatenate(partner, axis=0)], axis=1)
+    features = jnp.concatenate([piece[:, :rows] for piece in features], axis=0)
     both = lax.dot_general(features, keys, contract, preferred_element_type=jnp.float32)
     grads_ref[...] = both[:, :head_size] + both[:, head_size:]
 
@@ -159,19 +168,21 @@
     diagonal = rows == columns
     trace = jnp.sum(jnp.where(diagonal, gram, 0.0), axis=(0, 1), keepdims=True)
     inverse = 1.0 / (jnp.sqrt(trace) + epsilon)
-    gram = gram * (inverse * inverse)
+    scaling = inverse * inverse
     start = jnp.where(diagonal, first_coef, 0.0)
-    product = None
-    for _ in range(ITERS - 1):
+    split = thirds(gram)
+    square = product_of(split, split)
+    gram = gram * scaling
+    split = thirds(gram)
+    product = start + second_coef * gram + (third_coef * scaling) * (scaling * square)
+    factor = thirds(product)
+    gram = product_of(thirds(product_of(split, factor)), factor)
+    for _ in range(ITERS - 2):
         split = thirds(gram)
         square = product_of(split, split)
-        poly = start + second_coef * gram + third_coef * square
-        factor = thirds(poly)
-        if product is None:
-            product, turned = poly, product_of(split, factor)
-        else:
-            both = product_of(stacked(split, thirds(product)), factor)
-            turned, product = both[:size], both[size:]
+        factor = thirds(start + second_coef * gram + third_coef * square)
+        both = product_of(stacked(split, thirds(product)), factor)
+        turned, product = both[:size], both[size:]
         gram = product_of(thirds(turned), factor)
     split = thirds(gram)
     poly = start + second_coef * gram + third_coef * product_of(split, split)
@@ -204,37 +215,41 @@
     tokens, head_size = own_part.shape
     rows_half = moment.shape[0]
     bits = [1 << b for b in reversed(range(n_fsdp.bit_length() - 1))]
-    direct = n_fsdp == 1 << len(bits) and n_fsdp <= 8 and rows_half % 128 == 0 and n_tp & (n_tp - 1) == 0
+    direct = n_fsdp == 1 << len(bits) and 4 <= n_fsdp <= 8 and rows_half % 128 == 0 and n_tp & (n_tp - 1) == 0
     block = pltpu.VMEM((rows_half, head_size), jnp.float32)
     small = pltpu.VMEM((head_size // 2 + 8, head_size), jnp.float32)
     if direct:
         n_chip = n_fsdp // 2
-        gathered, stages = own_part, [own_part]
-        packed = pltpu.VMEM((tokens, 2 * rows_half), features.dtype)
-        for bit in bits[-2::-1]:
-            stages.append(swapped(gathered, bit, 0))
-            gathered = jnp.concatenate([gathered, stages[-1]], axis=0)
+        wide = 2 * rows_half
+        apart = [not d or far(d) for d in range(n_chip)]
+        packed = [pltpu.VMEM((tokens, wide if alone else wide + head_size), features.dtype) for alone in apart]
         pieces = pl.pallas_call(
             lambda *refs: pack_kernel(rows_half, *refs),
-            out_shape=(packed,) * n_chip,
-            in_specs=[pl.BlockSpec(memory_space=pl.ANY)],
+            out_shape=tuple(packed),
+            in_specs=[pl.BlockSpec(memory_space=pl.ANY)] * 2,
             out_specs=tuple(whole(n_chip)),
-            scratch_shapes=[pltpu.SemaphoreType.DMA((2 * n_chip,))],
+            scratch_shapes=[pltpu.SemaphoreType.DMA((3 * n_chip,))],
             name="pack",
-        )(features)
-        pieces = list(pieces)
+        )(features, own_part)
+        pieces, stages = list(pieces), [own_part]
         for d in range(1, n_chip):
-            pieces[d] = swapped(pieces[d], 2 * d, 0)
-        partner_keys = swapped(gathered, 0, 1)
+            pieces[d] = swapped(pieces[d], 2 * d, 0, 2 * turned(d, n_chip))
+            if apart[d]:
+                stages.append(swapped(own_part, 2 * d, 0, 2 * turned(d, n_chip)))
+        lone = list(stages)
+        keys = [lone.pop(0) if apart[d] else pieces[d][:, wide:] for d in range(n_chip)]
+        near_keys = jnp.concatenate([keys[d] for d in range(n_chip) if not far(d)], axis=0)
+        partner_keys = [swapped(near_keys, 0, 1)]
+        partner_keys += [swapped(keys[d], 0, 1) for d in range(n_chip) if far(d)]
         twin = swapped(moment, 1, 0)
-        partner_keys, twin = lax.optimization_barrier((partner_keys, twin))
+        partner_keys[0], twin = lax.optimization_barrier((partner_keys[0], twin))
         grads = pl.pallas_call(
             lambda *refs: partial_kernel(n_chip, *refs),
             out_shape=pltpu.VMEM((2 * rows_half, head_size), jnp.float32),
-            in_specs=whole(n_chip + len(stages) + 1),
+            in_specs=whole(n_chip + len(stages) + len(partner_keys)),
             out_specs=whole(1)[0],
             name="partial",
-        )(*on_chip(*pieces, *stages, partner_keys))
+        )(*on_chip(*pieces, *stages, *partner_keys))
         fresh, blend, gram = pl.pallas_call(
             joined_kernel,
             out_shape=(block, block, small),
@@ -244,7 +259,7 @@
         )(*on_chip(grads, swapped(grads, 1, 0), moment, twin))
         others = []
         for d in reversed(range(1, n_chip)):
-            others.append(swapped(gram, 2 * d, 0))
+            others.append(swapped(gram, 2 * d, 0, 2 * turned(d, n_chip)))
         for other in others:
             gram = gram + other
         grams = [gram, swapped(gram, 0, 1)]

time: 42.8 us -> 42.3 us (0.988)
  other arithmetic: 0.78 us -> 0.02 us
  starting transfers between devices: 15.5 us -> 16.2 us
  waiting for transfers between devices: 19.2 us -> 18.7 us
    concatenate x2 -> x1, other arithmetic: 0.77 us -> 0.01 us  [ordered(): jnp.concatenate([keys[d] for d in range(n_chip) if not far(d)], axis=0)]
    ppermute x12, starting transfers between devices: 15.5 us -> 16.2 us  [swapped(): lax.ppermute(block, ('fsdp', 'tp'), [(i, i ^ mask) for i, mask in enumera...]
  transfers between devices with their start and end apart: 12 -> 12, of which waited for: 9 -> 8; matrix products, arithmetic and copies ran while one was open for 2% -> 2% of each run, Pallas kernels for 3% -> 0%
where the time goes in v4:
time: 42.3 us; the launch traced here: 42.1 us
  waiting for transfers between devices  18.7 us (44%)
  starting transfers between devices  16.2 us (38%)
  Pallas kernels  5.73 us (14%)
  local copies, waits for them, and re-layouts  0.72 us (2%)
  between operations  0.7 us (2%)
    ppermute x12, waiting for transfers between devices, swapped(): lax.ppermute(block, ('fsdp', 'tp'), [(i, i ^ mask) for i, mask in enumera...  18.7 us
    ppermute x12, starting transfers between devices, swapped(): lax.ppermute(block, ('fsdp', 'tp'), [(i, i ^ mask) for i, mask in enumera...  16.2 us
    pallas_call x1, Pallas kernels, ordered(): pl.pallas_call(lambda *refs: newton_kernel(scale, len(grams), *refs), out...  3.23 us
    pallas_call x1, Pallas kernels, ordered(): pl.pallas_call(lambda *refs: pack_kernel(rows_half, *refs), out_shape=tup...  1.47 us
  transfers between devices with their start and end apart: 12, of which 8 were waited for; matrix products, arithmetic and copies ran while one was open for 2% of the time, Pallas kernels for 0%

profile of v4, /device:TPU:0, one launch (start us, length us, event | category | flops | bytes accessed | tf_op | source)
XLA Modules:
  0.0 42.1 jit_solution(7226507914114131012)
XLA Ops:
  0.6 0.0 copy-start
  0.6 0.0 copy-start.1
  0.6 1.5 %pack.1 = (bf16[128,1024]{1,0:T(8,128)(2,1)S(1)}, bf16[128,1152]{1,0:T(8,128)(2,1)S(1)}, bf16[128,1152]{1,0:T(8,128)(2,1)S(1)}, bf16[128,1024]{1,0:T(8,128)(2,1)S(1)}) custom-call(bf16[128,8192]{1,0:T(8,128)(2,1)} %refs_0_.1, bf16[128,128]{1,0:T(8,128)(2,1)} %bitcast.9), custom_call_target="tpu_custom_call" | custom-call | tf_op jit(solution)/shard_map/pack/pallas_call | solution.py:226
  2.1 3.0 %collective-permute-start = (bf16[128,1152]{1,0:T(8,128)(2,1)S(1)}, bf16[128,1152]{1,0:T(8,128)(2,1)S(1)}, u32[]{:S(2)}, u32[]{:S(2)}) collective-permute-start(bf16[128,1152]{1,0:T(8,128)(2,1)S(1)} %get-tuple-element.12), channel_id=1, source_target_pairs={{0,8},{1,9},{2,10},{3,11},{4,20},{5,21},{6,22},{7,23},{8,0},{9,1},... | collective-permute-start | bytes 884744 | tf_op jit(solution)/shard_map/ppermute | solution.py:28
  5.2 1.5 %collective-permute-start.1 = (bf16[128,1152]{1,0:T(8,128)(2,1)S(1)}, bf16[128,1152]{1,0:T(8,128)(2,1)S(1)}, u32[]{:S(2)}, u32[]{:S(2)}) collective-permute-start(bf16[128,1152]{1,0:T(8,128)(2,1)S(1)} %get-tuple-element.13), channel_id=1, source_target_pairs={{0,16},{1,17},{2,18},{3,19},{4,12},{5,13},{6,14},{7,15},{8,24},{9,... | collective-permute-start | bytes 884744 | tf_op jit(solution)/shard_map/ppermute | solution.py:28
  6.7 0.0 copy-done.1
  6.7 0.0 collective-permute-start.5
  6.7 0.0 collective-permute-start.2
  6.7 5.7 %collective-permute-done.refs_1_ = bf16[128,1152]{1,0:T(8,128)(2,1)S(1)} collective-permute-done((bf16[128,1152]{1,0:T(8,128)(2,1)S(1)}, bf16[128,1152]{1,0:T(8,128)(2,1)S(1)}, u32[]{:S(2)}, u32[]{:S(2)}) %collective-permute-start) | collective-permute-done | bytes 294944 | tf_op jit(solution)/shard_map/ppermute | solution.py:28
  12.5 0.0 collective-permute-done.1.refs_2_
  12.5 0.0 copy-done
  12.5 2.6 %collective-permute-start.4 = (bf16[384,128]{1,0:T(8,128)(2,1)S(1)}, bf16[384,128]{1,0:T(8,128)(2,1)S(1)}, u32[]{:S(2)}, u32[]{:S(2)}) collective-permute-start(bf16[384,128]{1,0:T(8,128)(2,1)S(1)} %pad_maximum_fusion), channel_id=1, source_target_pairs={{0,1},{1,0},{2,3},{3,2},{4,5},{5,4},{6,7},{7,6},{8,9},{9,8},{10,11... | collective-permute-start | bytes 294920 | tf_op jit(solution)/shard_map/ppermute | solution.py:28
  15.1 2.6 %collective-permute-start.3 = (bf16[128,128]{1,0:T(8,128)(2,1)S(1)}, bf16[128,128]{1,0:T(8,128)(2,1)S(1)}, u32[]{:S(2)}, u32[]{:S(2)}) collective-permute-start(bf16[128,128]{1,0:T(8,128)(2,1)S(1)} %bitcast.11), channel_id=1, source_target_pairs={{0,24},{1,25},{2,26},{3,27},{4,28},{5,29},{6,30},{7,31},{8,16},{9,... | collective-permute-start | bytes 98312 | tf_op jit(solution)/shard_map/ppermute | solution.py:28
  17.7 2.3 %collective-permute-done.3.refs_5_ = bf16[128,128]{1,0:T(8,128)(2,1)S(1)} collective-permute-done((bf16[128,128]{1,0:T(8,128)(2,1)S(1)}, bf16[128,128]{1,0:T(8,128)(2,1)S(1)}, u32[]{:S(2)}, u32[]{:S(2)}) %collective-permute-start.3) | collective-permute-done | bytes 32800 | tf_op jit(solution)/shard_map/ppermute | solution.py:28
  19.9 1.6 %collective-permute-start.6 = (bf16[128,128]{1,0:T(8,128)(2,1)S(1)}, bf16[128,128]{1,0:T(8,128)(2,1)S(1)}, u32[]{:S(2)}, u32[]{:S(2)}) collective-permute-start(bf16[128,128]{1,0:T(8,128)(2,1)S(1)} %collective-permute-done.3.refs_5_), channel_id=1, source_target_pairs={{0,1},{1,0},{2,3},{3,2},{4,5},{5,4},{6,7},{7,6},{8,9},{9,8},{10,11... | collective-permute-start | bytes 98312 | tf_op jit(solution)/shard_map/ppermute | solution.py:28
  21.5 0.0 collective-permute-done.5.twin_ref
  21.5 0.0 collective-permute-done.4.refs_6_
  21.5 2.4 %collective-permute-done.6.refs_7_ = bf16[128,128]{1,0:T(8,128)(2,1)S(1)} collective-permute-done((bf16[128,128]{1,0:T(8,128)(2,1)S(1)}, bf16[128,128]{1,0:T(8,128)(2,1)S(1)}, u32[]{:S(2)}, u32[]{:S(2)}) %collective-permute-start.6) | collective-permute-done | bytes 32800 | tf_op jit(solution)/shard_map/ppermute | solution.py:28
  23.9 0.0 collective-permute-done.2.refs_3_
  23.9 0.5 %partial.1.own_ref = f32[1024,128]{1,0:T(8,128)S(1)} custom-call(bf16[128,1024]{1,0:T(8,128)(2,1)S(1)} %get-tuple-element.11.refs_0_, bf16[128,1152]{1,0:T(8,128)(2,1)S(1)} %collective-permute-done.refs_1_, bf16[128,1152]{1,0:T(8,128)(2,1)S(1)} %collective-permute-done.1.refs_2_, bf16[128,1024]{1,0:T(8,128)(2,1)S(1)} %collective-permute-done.2.refs_3_, ...), custom_call_target="tpu_custom_call" | custom-call | tf_op jit(solution)/shard_map/partial/pallas_call | solution.py:246
  24.4 0.1 collective-permute-start.7
  24.4 1.9 %collective-permute-done.7.other_ref = f32[1024,128]{1,0:T(8,128)S(1)} collective-permute-done((f32[1024,128]{1,0:T(8,128)S(1)}, f32[1024,128]{1,0:T(8,128)S(1)}, u32[]{:S(2)}, u32[]{:S(2)}) %collective-permute-start.7) | collective-permute-done | bytes 524320 | tf_op jit(solution)/shard_map/ppermute | solution.py:28
  26.3 0.5 %gradient.1 = (f32[512,128]{1,0:T(8,128)S(1)}, f32[512,128]{1,0:T(8,128)S(1)}, f32[72,128]{1,0:T(8,128)S(1)}) custom-call(f32[1024,128]{1,0:T(8,128)S(1)} %partial.1.own_ref, f32[1024,128]{1,0:T(8,128)S(1)} %collective-permute-done.7.other_ref, f32[512,128]{1,0:T(8,128)S(1)} %bitcast.14, f32[512,128]{1,0:T(8,128)S(1)} %collective-permute-done.5.twin_ref), custom_call_target="tpu_custom_call" | custom-call | tf_op jit(solution)/shard_map/gradient/pallas_call | solution.py:253
  26.9 1.5 %collective-permute-start.10 = (f32[72,128]{1,0:T(8,128)S(1)}, f32[72,128]{1,0:T(8,128)S(1)}, u32[]{:S(2)}, u32[]{:S(2)}) collective-permute-start(f32[72,128]{1,0:T(8,128)S(1)} %get-tuple-element.17), channel_id=1, source_target_pairs={{0,8},{1,9},{2,10},{3,11},{4,20},{5,21},{6,22},{7,23},{8,0},{9,1},... | collective-permute-start | bytes 110600 | tf_op jit(solution)/shard_map/ppermute | solution.py:28
  28.4 1.6 %collective-permute-start.9 = (f32[72,128]{1,0:T(8,128)S(1)}, f32[72,128]{1,0:T(8,128)S(1)}, u32[]{:S(2)}, u32[]{:S(2)}) collective-permute-start(f32[72,128]{1,0:T(8,128)S(1)} %get-tuple-element.17), channel_id=1, source_target_pairs={{0,16},{1,17},{2,18},{3,19},{4,12},{5,13},{6,14},{7,15},{8,24},{9,... | collective-permute-start | bytes 110600 | tf_op jit(solution)/shard_map/ppermute | solution.py:28
  30.0 0.4 collective-permute-start.8
  30.4 0.5 %collective-permute-done.10 = f32[72,128]{1,0:T(8,128)S(1)} collective-permute-done((f32[72,128]{1,0:T(8,128)S(1)}, f32[72,128]{1,0:T(8,128)S(1)}, u32[]{:S(2)}, u32[]{:S(2)}) %collective-permute-start.10) | collective-permute-done | bytes 36896 | tf_op jit(solution)/shard_map/ppermute | solution.py:28
  30.8 1.5 %collective-permute-done.9 = f32[72,128]{1,0:T(8,128)S(1)} collective-permute-done((f32[72,128]{1,0:T(8,128)S(1)}, f32[72,128]{1,0:T(8,128)S(1)}, u32[]{:S(2)}, u32[]{:S(2)}) %collective-permute-start.9) | collective-permute-done | bytes 36896 | tf_op jit(solution)/shard_map/ppermute | solution.py:28
  32.3 2.5 %collective-permute-done.8 = f32[72,128]{1,0:T(8,128)S(1)} collective-permute-done((f32[72,128]{1,0:T(8,128)S(1)}, f32[72,128]{1,0:T(8,128)S(1)}, u32[]{:S(2)}, u32[]{:S(2)}) %collective-permute-start.8) | collective-permute-done | bytes 36896 | tf_op jit(solution)/shard_map/ppermute | solution.py:28
  34.9 1.3 %collective-permute-start.11 = (f32[72,128]{1,0:T(8,128)S(1)}, f32[72,128]{1,0:T(8,128)S(1)}, u32[]{:S(2)}, u32[]{:S(2)}) collective-permute-start(f32[72,128]{1,0:T(8,128)S(1)} %add_add_fusion.refs_0_), channel_id=1, source_target_pairs={{0,1},{1,0},{2,3},{3,2},{4,5},{5,4},{6,7},{7,6},{8,9},{9,8},{10,11... | collective-permute-start | bytes 110600 | tf_op jit(solution)/shard_map/ppermute | solution.py:28
  36.2 0.7 %copy.7 = f32[512,1,128]{2,1,0:T(1,128)} copy(f32[512,1,128]{2,1,0:T(1,128)S(1)} %bitcast.8) | data formatting | bytes 524288
  36.9 2.0 %collective-permute-done.11.refs_1_ = f32[72,128]{1,0:T(8,128)S(1)} collective-permute-done((f32[72,128]{1,0:T(8,128)S(1)}, f32[72,128]{1,0:T(8,128)S(1)}, u32[]{:S(2)}, u32[]{:S(2)}) %collective-permute-start.11) | collective-permute-done | bytes 36896 | tf_op jit(solution)/shard_map/ppermute | solution.py:28
  38.9 3.2 %newton.1 = f32[512,128]{1,0:T(8,128)} custom-call(f32[72,128]{1,0:T(8,128)S(1)} %add_add_fusion.refs_0_, f32[72,128]{1,0:T(8,128)S(1)} %collective-permute-done.11.refs_1_, f32[512,128]{1,0:T(8,128)S(1)} %get-tuple-element.18.refs_2_), custom_call_target="tpu_custom_call" | custom-call | tf_op jit(solution)/shard_map/newton/pallas_call | solution.py:286
  (4 shorter events, 0.0 us)
Async XLA Ops:
  0.6 11.8 %copy-start = (bf16[128,1,128]{2,0,1:T(8,128)(2,1)S(1)}, bf16[128,1,128]{2,0,1:T(8,128)(2,1)}, u32[]{:S(2)}) copy-start(bf16[128,1,128]{2,0,1:T(8,128)(2,1)} %param.4) | copy-start | bytes 98308
  0.6 6.0 %copy-start.1 = (f32[512,1,128]{2,1,0:T(1,128)S(1)}, f32[512,1,128]{2,1,0:T(1,128)}, u32[]{:S(2)}) copy-start(f32[512,1,128]{2,1,0:T(1,128)} %param.5) | copy-start | bytes 786436
  2.1 10.3 %collective-permute-start = (bf16[128,1152]{1,0:T(8,128)(2,1)S(1)}, bf16[128,1152]{1,0:T(8,128)(2,1)S(1)}, u32[]{:S(2)}, u32[]{:S(2)}) collective-permute-start(bf16[128,1152]{1,0:T(8,128)(2,1)S(1)} %get-tuple-element.12), channel_id=1, source_target_pairs={{0,8},{1,9},{2,10},{3,11},{4,20},{5,21},{6,22},{7,23},{8,0},{9,1},... | collective-permute-start | bytes 884744 | tf_op jit(solution)/shard_map/ppermute | solution.py:28
  5.2 7.3 %collective-permute-start.1 = (bf16[128,1152]{1,0:T(8,128)(2,1)S(1)}, bf16[128,1152]{1,0:T(8,128)(2,1)S(1)}, u32[]{:S(2)}, u32[]{:S(2)}) collective-permute-start(bf16[128,1152]{1,0:T(8,128)(2,1)S(1)} %get-tuple-element.13), channel_id=1, source_target_pairs={{0,16},{1,17},{2,18},{3,19},{4,12},{5,13},{6,14},{7,15},{8,24},{9,... | collective-permute-start | bytes 884744 | tf_op jit(solution)/shard_map/ppermute | solution.py:28
  6.7 14.8 %collective-permute-start.5 = (f32[512,128]{1,0:T(8,128)S(1)}, f32[512,128]{1,0:T(8,128)S(1)}, u32[]{:S(2)}, u32[]{:S(2)}) collective-permute-start(f32[512,128]{1,0:T(8,128)S(1)} %bitcast.13), channel_id=1, source_target_pairs={{0,4},{1,5},{2,6},{3,7},{4,0},{5,1},{6,2},{7,3},{8,12},{9,13},{10,... | collective-permute-start | bytes 786440 | tf_op jit(solution)/shard_map/ppermute | solution.py:28
  6.7 17.2 %collective-permute-start.2 = (bf16[128,1024]{1,0:T(8,128)(2,1)S(1)}, bf16[128,1024]{1,0:T(8,128)(2,1)S(1)}, u32[]{:S(2)}, u32[]{:S(2)}) collective-permute-start(bf16[128,1024]{1,0:T(8,128)(2,1)S(1)} %get-tuple-element.14), channel_id=1, source_target_pairs={{0,24},{1,25},{2,26},{3,27},{4,28},{5,29},{6,30},{7,31},{8,16},{9,... | collective-permute-start | bytes 786440 | tf_op jit(solution)/shard_map/ppermute | solution.py:28
  12.5 9.0 %collective-permute-start.4 = (bf16[384,128]{1,0:T(8,128)(2,1)S(1)}, bf16[384,128]{1,0:T(8,128)(2,1)S(1)}, u32[]{:S(2)}, u32[]{:S(2)}) collective-permute-start(bf16[384,128]{1,0:T(8,128)(2,1)S(1)} %pad_maximum_fusion), channel_id=1, source_target_pairs={{0,1},{1,0},{2,3},{3,2},{4,5},{5,4},{6,7},{7,6},{8,9},{9,8},{10,11... | collective-permute-start | bytes 294920 | tf_op jit(solution)/shard_map/ppermute | solution.py:28
  15.1 4.8 %collective-permute-start.3 = (bf16[128,128]{1,0:T(8,128)(2,1)S(1)}, bf16[128,128]{1,0:T(8,128)(2,1)S(1)}, u32[]{:S(2)}, u32[]{:S(2)}) collective-permute-start(bf16[128,128]{1,0:T(8,128)(2,1)S(1)} %bitcast.11), channel_id=1, source_target_pairs={{0,24},{1,25},{2,26},{3,27},{4,28},{5,29},{6,30},{7,31},{8,16},{9,... | collective-permute-start | bytes 98312 | tf_op jit(solution)/shard_map/ppermute | solution.py:28
  19.9 3.9 %collective-permute-start.6 = (bf16[128,128]{1,0:T(8,128)(2,1)S(1)}, bf16[128,128]{1,0:T(8,128)(2,1)S(1)}, u32[]{:S(2)}, u32[]{:S(2)}) collective-permute-start(bf16[128,128]{1,0:T(8,128)(2,1)S(1)} %collective-permute-done.3.refs_5_), channel_id=1, source_target_pairs={{0,1},{1,0},{2,3},{3,2},{4,5},{5,4},{6,7},{7,6},{8,9},{9,8},{10,11... | collective-permute-start | bytes 98312 | tf_op jit(solution)/shard_map/ppermute | solution.py:28
  24.4 2.0 %collective-permute-start.7 = (f32[1024,128]{1,0:T(8,128)S(1)}, f32[1024,128]{1,0:T(8,128)S(1)}, u32[]{:S(2)}, u32[]{:S(2)}) collective-permute-start(f32[1024,128]{1,0:T(8,128)S(1)} %partial.1.own_ref), channel_id=1, source_target_pairs={{0,4},{1,5},{2,6},{3,7},{4,0},{5,1},{6,2},{7,3},{8,12},{9,13},{10,... | collective-permute-start | bytes 1572872 | tf_op jit(solution)/shard_map/ppermute | solution.py:28
  26.9 4.0 %collective-permute-start.10 = (f32[72,128]{1,0:T(8,128)S(1)}, f32[72,128]{1,0:T(8,128)S(1)}, u32[]{:S(2)}, u32[]{:S(2)}) collective-permute-start(f32[72,128]{1,0:T(8,128)S(1)} %get-tuple-element.17), channel_id=1, source_target_pairs={{0,8},{1,9},{2,10},{3,11},{4,20},{5,21},{6,22},{7,23},{8,0},{9,1},... | collective-permute-start | bytes 110600 | tf_op jit(solution)/shard_map/ppermute | solution.py:28
  28.4 4.0 %collective-permute-start.9 = (f32[72,128]{1,0:T(8,128)S(1)}, f32[72,128]{1,0:T(8,128)S(1)}, u32[]{:S(2)}, u32[]{:S(2)}) collective-permute-start(f32[72,128]{1,0:T(8,128)S(1)} %get-tuple-element.17), channel_id=1, source_target_pairs={{0,16},{1,17},{2,18},{3,19},{4,12},{5,13},{6,14},{7,15},{8,24},{9,... | collective-permute-start | bytes 110600 | tf_op jit(solution)/shard_map/ppermute | solution.py:28
  30.0 4.9 %collective-permute-start.8 = (f32[72,128]{1,0:T(8,128)S(1)}, f32[72,128]{1,0:T(8,128)S(1)}, u32[]{:S(2)}, u32[]{:S(2)}) collective-permute-start(f32[72,128]{1,0:T(8,128)S(1)} %get-tuple-element.17), channel_id=1, source_target_pairs={{0,24},{1,25},{2,26},{3,27},{4,28},{5,29},{6,30},{7,31},{8,16},{9,... | collective-permute-start | bytes 110600 | tf_op jit(solution)/shard_map/ppermute | solution.py:28
  34.9 4.0 %collective-permute-start.11 = (f32[72,128]{1,0:T(8,128)S(1)}, f32[72,128]{1,0:T(8,128)S(1)}, u32[]{:S(2)}, u32[]{:S(2)}) collective-permute-start(f32[72,128]{1,0:T(8,128)S(1)} %add_add_fusion.refs_0_), channel_id=1, source_target_pairs={{0,1},{1,0},{2,3},{3,2},{4,5},{5,4},{6,7},{7,6},{8,9},{9,8},{10,11... | collective-permute-start | bytes 110600 | tf_op jit(solution)/shard_map/ppermute | solution.py:28

commit v5 on v4

--- a/solution.py
+++ b/solution.py
@@ -96,14 +96,14 @@
     return distance & (distance - 1) != 0
 
 
-def pack_kernel(width, features_ref, keys_ref, *refs):
+def pack_kernel(width, n_chip, slots, features_ref, keys_ref, *refs):
     outs, sems = refs[:-1], refs[-1]
     index = lax.axis_index("fsdp")
     parity = lax.axis_index("tp") % 2
     chip, core = index // 2, index % 2
     copies = []
-    for i, out in enumerate(outs):
-        distance = jnp.where(core == 0, i, turned(i, len(outs)))
+    for i, out in zip(slots, outs):
+        distance = jnp.where(core == 0, i, turned(i, n_chip))
         for j in range(2):
             block = (chip ^ distance) * 2 + (core ^ j)
             start = pl.multiple_of((block * 2 + parity) * width, width)
@@ -223,15 +223,20 @@
         wide = 2 * rows_half
         apart = [not d or far(d) for d in range(n_chip)]
         packed = [pltpu.VMEM((tokens, wide if alone else wide + head_size), features.dtype) for alone in apart]
-        pieces = pl.pallas_call(
-            lambda *refs: pack_kernel(rows_half, *refs),
-            out_shape=tuple(packed),
-            in_specs=[pl.BlockSpec(memory_space=pl.ANY)] * 2,
-            out_specs=tuple(whole(n_chip)),
-            scratch_shapes=[pltpu.SemaphoreType.DMA((3 * n_chip,))],
-            name="pack",
-        )(features, own_part)
-        pieces, stages = list(pieces), [own_part]
+        pieces = [None] * n_chip
+        for slots in ([1], [2], list(range(3, n_chip)), [0]):
+            if not slots:
+                continue
+            arrays = pl.pallas_call(
+                lambda *refs, slots=slots: pack_kernel(rows_half, n_chip, slots, *refs),
+                out_shape=tuple(packed[d] for d in slots),
+                in_specs=[pl.BlockSpec(memory_space=pl.ANY)] * 2,
+                out_specs=tuple(whole(len(slots))),
+                scratch_shapes=[pltpu.SemaphoreType.DMA((3 * len(slots),))],
+            )(features, own_part)
+            for d, array in zip(slots, arrays):
+                pieces[d] = array
+        stages = [own_part]
         for d in range(1, n_chip):
             pieces[d] = swapped(pieces[d], 2 * d, 0, 2 * turned(d, n_chip))
             if apart[d]:

time: 42.3 us -> 41.7 us (0.986)
  Pallas kernels: 5.73 us -> 8.31 us
  waiting for transfers between devices: 18.7 us -> 16.5 us
  starting transfers between devices: 16.2 us -> 15.2 us
    pallas_call x1 -> x4, Pallas kernels: 1.47 us -> 4.06 us  [ordered(): pl.pallas_call(lambda *refs, slots=slots: pack_kernel(rows_half, n_chip,...]
    ppermute x12, waiting for transfers between devices: 18.7 us -> 16.5 us  [swapped(): lax.ppermute(block, ('fsdp', 'tp'), [(i, i ^ mask) for i, mask in enumera...]
    ppermute x12, starting transfers between devices: 16.2 us -> 15.2 us  [swapped(): lax.ppermute(block, ('fsdp', 'tp'), [(i, i ^ mask) for i, mask in enumera...]
  transfers between devices with their start and end apart: 12 -> 12, of which waited for: 8 -> 9; matrix products, arithmetic and copies ran while one was open for 2% -> 2% of each run, Pallas kernels for 0% -> 7%
where the time goes in v5:
time: 41.7 us; the launch traced here: 41.5 us
  waiting for transfers between devices  16.5 us (40%)
  starting transfers between devices  15.2 us (36%)
  Pallas kernels  8.31 us (20%)
  local copies, waits for them, and re-layouts  0.72 us (2%)
  between operations  0.72 us (2%)
    ppermute x12, waiting for transfers between devices, swapped(): lax.ppermute(block, ('fsdp', 'tp'), [(i, i ^ mask) for i, mask in enumera...  16.5 us
    ppermute x12, starting transfers between devices, swapped(): lax.ppermute(block, ('fsdp', 'tp'), [(i, i ^ mask) for i, mask in enumera...  15.2 us
    pallas_call x4, Pallas kernels, ordered(): pl.pallas_call(lambda *refs, slots=slots: pack_kernel(rows_half, n_chip,...  4.06 us
    pallas_call x1, Pallas kernels, ordered(): pl.pallas_call(lambda *refs: newton_kernel(scale, len(grams), *refs), out...  3.23 us
  transfers between devices with their start and end apart: 12, of which 9 were waited for; matrix products, arithmetic and copies ran while one was open for 2% of the time, Pallas kernels for 7%

profile of v5, /device:TPU:0, one launch (start us, length us, event | category | flops | bytes accessed | tf_op | source)
XLA Modules:
  0.0 41.5 jit_solution(18087322954719630673)
XLA Ops:
  0.6 0.0 copy-start.2
  0.6 1.1 %shard_map.51 = bf16[128,1152]{1,0:T(8,128)(2,1)S(1)} custom-call(bf16[128,8192]{1,0:T(8,128)(2,1)} %refs_0_.7, bf16[128,128]{1,0:T(8,128)(2,1)} %bitcast.9), custom_call_target="tpu_custom_call" | custom-call | tf_op jit(solution)/shard_map/pallas_call | solution.py:230
  1.7 0.0 copy-start
  1.7 3.0 %collective-permute-start = (bf16[128,1152]{1,0:T(8,128)(2,1)S(1)}, bf16[128,1152]{1,0:T(8,128)(2,1)S(1)}, u32[]{:S(2)}, u32[]{:S(2)}) collective-permute-start(bf16[128,1152]{1,0:T(8,128)(2,1)S(1)} %shard_map.51), channel_id=1, source_target_pairs={{0,8},{1,9},{2,10},{3,11},{4,20},{5,21},{6,22},{7,23},{8,0},{9,1},... | collective-permute-start | bytes 884744 | tf_op jit(solution)/shard_map/ppermute | solution.py:28
  4.7 1.0 %shard_map.52 = bf16[128,1152]{1,0:T(8,128)(2,1)S(1)} custom-call(bf16[128,8192]{1,0:T(8,128)(2,1)} %refs_0_.7, bf16[128,128]{1,0:T(8,128)(2,1)} %bitcast.10), custom_call_target="tpu_custom_call" | custom-call | tf_op jit(solution)/shard_map/pallas_call | solution.py:230
  5.8 1.6 %collective-permute-start.1 = (bf16[128,1152]{1,0:T(8,128)(2,1)S(1)}, bf16[128,1152]{1,0:T(8,128)(2,1)S(1)}, u32[]{:S(2)}, u32[]{:S(2)}) collective-permute-start(bf16[128,1152]{1,0:T(8,128)(2,1)S(1)} %shard_map.52), channel_id=1, source_target_pairs={{0,16},{1,17},{2,18},{3,19},{4,12},{5,13},{6,14},{7,15},{8,24},{9,... | collective-permute-start | bytes 884744 | tf_op jit(solution)/shard_map/ppermute | solution.py:28
  7.3 0.0 copy-done.2
  7.3 0.0 copy-start.1
  7.3 0.0 collective-permute-start.5
  7.3 1.0 %shard_map.53 = bf16[128,1024]{1,0:T(8,128)(2,1)S(1)} custom-call(bf16[128,8192]{1,0:T(8,128)(2,1)} %refs_0_.7, bf16[128,128]{1,0:T(8,128)(2,1)} %bitcast.11), custom_call_target="tpu_custom_call" | custom-call | tf_op jit(solution)/shard_map/pallas_call | solution.py:230
  8.4 0.1 collective-permute-start.2
  8.5 2.5 %collective-permute-done.refs_1_ = bf16[128,1152]{1,0:T(8,128)(2,1)S(1)} collective-permute-done((bf16[128,1152]{1,0:T(8,128)(2,1)S(1)}, bf16[128,1152]{1,0:T(8,128)(2,1)S(1)}, u32[]{:S(2)}, u32[]{:S(2)}) %collective-permute-start) | collective-permute-done | bytes 294944 | tf_op jit(solution)/shard_map/ppermute | solution.py:28
  11.0 1.6 %collective-permute-done.1.refs_2_ = bf16[128,1152]{1,0:T(8,128)(2,1)S(1)} collective-permute-done((bf16[128,1152]{1,0:T(8,128)(2,1)S(1)}, bf16[128,1152]{1,0:T(8,128)(2,1)S(1)}, u32[]{:S(2)}, u32[]{:S(2)}) %collective-permute-start.1) | collective-permute-done | bytes 294944 | tf_op jit(solution)/shard_map/ppermute | solution.py:28
  12.5 0.0 copy-done
  12.6 1.6 %collective-permute-start.4 = (bf16[384,128]{1,0:T(8,128)(2,1)S(1)}, bf16[384,128]{1,0:T(8,128)(2,1)S(1)}, u32[]{:S(2)}, u32[]{:S(2)}) collective-permute-start(bf16[384,128]{1,0:T(8,128)(2,1)S(1)} %pad_maximum_fusion), channel_id=1, source_target_pairs={{0,1},{1,0},{2,3},{3,2},{4,5},{5,4},{6,7},{7,6},{8,9},{9,8},{10,11... | collective-permute-start | bytes 294920 | tf_op jit(solution)/shard_map/ppermute | solution.py:28
  14.2 2.9 %collective-permute-start.3 = (bf16[128,128]{1,0:T(8,128)(2,1)S(1)}, bf16[128,128]{1,0:T(8,128)(2,1)S(1)}, u32[]{:S(2)}, u32[]{:S(2)}) collective-permute-start(bf16[128,128]{1,0:T(8,128)(2,1)S(1)} %bitcast.14), channel_id=1, source_target_pairs={{0,24},{1,25},{2,26},{3,27},{4,28},{5,29},{6,30},{7,31},{8,16},{9,... | collective-permute-start | bytes 98312 | tf_op jit(solution)/shard_map/ppermute | solution.py:28
  17.1 3.3 %collective-permute-done.3.refs_5_ = bf16[128,128]{1,0:T(8,128)(2,1)S(1)} collective-permute-done((bf16[128,128]{1,0:T(8,128)(2,1)S(1)}, bf16[128,128]{1,0:T(8,128)(2,1)S(1)}, u32[]{:S(2)}, u32[]{:S(2)}) %collective-permute-start.3) | collective-permute-done | bytes 32800 | tf_op jit(solution)/shard_map/ppermute | solution.py:28
  20.4 1.4 %collective-permute-start.6 = (bf16[128,128]{1,0:T(8,128)(2,1)S(1)}, bf16[128,128]{1,0:T(8,128)(2,1)S(1)}, u32[]{:S(2)}, u32[]{:S(2)}) collective-permute-start(bf16[128,128]{1,0:T(8,128)(2,1)S(1)} %collective-permute-done.3.refs_5_), channel_id=1, source_target_pairs={{0,1},{1,0},{2,3},{3,2},{4,5},{5,4},{6,7},{7,6},{8,9},{9,8},{10,11... | collective-permute-start | bytes 98312 | tf_op jit(solution)/shard_map/ppermute | solution.py:28
  21.8 1.0 %shard_map.50.refs_0_ = bf16[128,1024]{1,0:T(8,128)(2,1)S(1)} custom-call(bf16[128,8192]{1,0:T(8,128)(2,1)} %refs_0_.7, bf16[128,128]{1,0:T(8,128)(2,1)} %bitcast.12), custom_call_target="tpu_custom_call" | custom-call | tf_op jit(solution)/shard_map/pallas_call | solution.py:230
  22.8 0.0 collective-permute-done.5.twin_ref
  22.8 0.0 collective-permute-done.4.refs_6_
  22.9 1.5 %collective-permute-done.6.refs_7_ = bf16[128,128]{1,0:T(8,128)(2,1)S(1)} collective-permute-done((bf16[128,128]{1,0:T(8,128)(2,1)S(1)}, bf16[128,128]{1,0:T(8,128)(2,1)S(1)}, u32[]{:S(2)}, u32[]{:S(2)}) %collective-permute-start.6) | collective-permute-done | bytes 32800 | tf_op jit(solution)/shard_map/ppermute | solution.py:28
  24.3 0.0 collective-permute-done.2.refs_3_
  24.3 0.0 copy-done.1
  24.3 0.5 %partial.1.own_ref = f32[1024,128]{1,0:T(8,128)S(1)} custom-call(bf16[128,1024]{1,0:T(8,128)(2,1)S(1)} %shard_map.50.refs_0_, bf16[128,1152]{1,0:T(8,128)(2,1)S(1)} %collective-permute-done.refs_1_, bf16[128,1152]{1,0:T(8,128)(2,1)S(1)} %collective-permute-done.1.refs_2_, bf16[128,1024]{1,0:T(8,128)(2,1)S(1)} %collective-permute-done.2.refs_3_, ...), custom_call_target="tpu_custom_call" | custom-call | tf_op jit(solution)/shard_map/partial/pallas_call | solution.py:251
  24.8 0.1 collective-permute-start.7
  24.9 1.9 %collective-permute-done.7.other_ref = f32[1024,128]{1,0:T(8,128)S(1)} collective-permute-done((f32[1024,128]{1,0:T(8,128)S(1)}, f32[1024,128]{1,0:T(8,128)S(1)}, u32[]{:S(2)}, u32[]{:S(2)}) %collective-permute-start.7) | collective-permute-done | bytes 524320 | tf_op jit(solution)/shard_map/ppermute | solution.py:28
  26.8 0.5 %gradient.1 = (f32[512,128]{1,0:T(8,128)S(1)}, f32[512,128]{1,0:T(8,128)S(1)}, f32[72,128]{1,0:T(8,128)S(1)}) custom-call(f32[1024,128]{1,0:T(8,128)S(1)} %partial.1.own_ref, f32[1024,128]{1,0:T(8,128)S(1)} %collective-permute-done.7.other_ref, f32[512,128]{1,0:T(8,128)S(1)} %bitcast.17, f32[512,128]{1,0:T(8,128)S(1)} %collective-permute-done.5.twin_ref), custom_call_target="tpu_custom_call" | custom-call | tf_op jit(solution)/shard_map/gradient/pallas_call | solution.py:258
  27.3 1.4 %collective-permute-start.10 = (f32[72,128]{1,0:T(8,128)S(1)}, f32[72,128]{1,0:T(8,128)S(1)}, u32[]{:S(2)}, u32[]{:S(2)}) collective-permute-start(f32[72,128]{1,0:T(8,128)S(1)} %get-tuple-element.9), channel_id=1, source_target_pairs={{0,8},{1,9},{2,10},{3,11},{4,20},{5,21},{6,22},{7,23},{8,0},{9,1},... | collective-permute-start | bytes 110600 | tf_op jit(solution)/shard_map/ppermute | solution.py:28
  28.7 0.7 %collective-permute-start.9 = (f32[72,128]{1,0:T(8,128)S(1)}, f32[72,128]{1,0:T(8,128)S(1)}, u32[]{:S(2)}, u32[]{:S(2)}) collective-permute-start(f32[72,128]{1,0:T(8,128)S(1)} %get-tuple-element.9), channel_id=1, source_target_pairs={{0,16},{1,17},{2,18},{3,19},{4,12},{5,13},{6,14},{7,15},{8,24},{9,... | collective-permute-start | bytes 110600 | tf_op jit(solution)/shard_map/ppermute | solution.py:28
  29.4 1.4 %collective-permute-start.8 = (f32[72,128]{1,0:T(8,128)S(1)}, f32[72,128]{1,0:T(8,128)S(1)}, u32[]{:S(2)}, u32[]{:S(2)}) collective-permute-start(f32[72,128]{1,0:T(8,128)S(1)} %get-tuple-element.9), channel_id=1, source_target_pairs={{0,24},{1,25},{2,26},{3,27},{4,28},{5,29},{6,30},{7,31},{8,16},{9,... | collective-permute-start | bytes 110600 | tf_op jit(solution)/shard_map/ppermute | solution.py:28
  30.8 0.5 %collective-permute-done.10 = f32[72,128]{1,0:T(8,128)S(1)} collective-permute-done((f32[72,128]{1,0:T(8,128)S(1)}, f32[72,128]{1,0:T(8,128)S(1)}, u32[]{:S(2)}, u32[]{:S(2)}) %collective-permute-start.10) | collective-permute-done | bytes 36896 | tf_op jit(solution)/shard_map/ppermute | solution.py:28
  31.3 1.7 %collective-permute-done.9 = f32[72,128]{1,0:T(8,128)S(1)} collective-permute-done((f32[72,128]{1,0:T(8,128)S(1)}, f32[72,128]{1,0:T(8,128)S(1)}, u32[]{:S(2)}, u32[]{:S(2)}) %collective-permute-start.9) | collective-permute-done | bytes 36896 | tf_op jit(solution)/shard_map/ppermute | solution.py:28
  33.0 1.2 %collective-permute-done.8 = f32[72,128]{1,0:T(8,128)S(1)} collective-permute-done((f32[72,128]{1,0:T(8,128)S(1)}, f32[72,128]{1,0:T(8,128)S(1)}, u32[]{:S(2)}, u32[]{:S(2)}) %collective-permute-start.8) | collective-permute-done | bytes 36896 | tf_op jit(solution)/shard_map/ppermute | solution.py:28
  34.3 0.9 %collective-permute-start.11 = (f32[72,128]{1,0:T(8,128)S(1)}, f32[72,128]{1,0:T(8,128)S(1)}, u32[]{:S(2)}, u32[]{:S(2)}) collective-permute-start(f32[72,128]{1,0:T(8,128)S(1)} %add_add_fusion.refs_0_), channel_id=1, source_target_pairs={{0,1},{1,0},{2,3},{3,2},{4,5},{5,4},{6,7},{7,6},{8,9},{9,8},{10,11... | collective-permute-start | bytes 110600 | tf_op jit(solution)/shard_map/ppermute | solution.py:28
  35.2 0.7 %copy.7 = f32[512,1,128]{2,1,0:T(1,128)} copy(f32[512,1,128]{2,1,0:T(1,128)S(1)} %bitcast.8) | data formatting | bytes 524288
  35.9 2.4 %collective-permute-done.11.refs_1_ = f32[72,128]{1,0:T(8,128)S(1)} collective-permute-done((f32[72,128]{1,0:T(8,128)S(1)}, f32[72,128]{1,0:T(8,128)S(1)}, u32[]{:S(2)}, u32[]{:S(2)}) %collective-permute-start.11) | collective-permute-done | bytes 36896 | tf_op jit(solution)/shard_map/ppermute | solution.py:28
  38.3 3.2 %newton.1 = f32[512,128]{1,0:T(8,128)} custom-call(f32[72,128]{1,0:T(8,128)S(1)} %add_add_fusion.refs_0_, f32[72,128]{1,0:T(8,128)S(1)} %collective-permute-done.11.refs_1_, f32[512,128]{1,0:T(8,128)S(1)} %get-tuple-element.10.refs_2_), custom_call_target="tpu_custom_call" | custom-call | tf_op jit(solution)/shard_map/newton/pallas_call | solution.py:291
  (4 shorter events, 0.0 us)
Async XLA Ops:
  0.6 6.7 %copy-start.2 = (f32[512,1,128]{2,1,0:T(1,128)S(1)}, f32[512,1,128]{2,1,0:T(1,128)}, u32[]{:S(2)}) copy-start(f32[512,1,128]{2,1,0:T(1,128)} %param.5) | copy-start | bytes 786436
  1.7 10.8 %copy-start = (bf16[128,1,128]{2,0,1:T(8,128)(2,1)S(1)}, bf16[128,1,128]{2,0,1:T(8,128)(2,1)}, u32[]{:S(2)}) copy-start(bf16[128,1,128]{2,0,1:T(8,128)(2,1)} %param.4) | copy-start | bytes 98308
  1.7 9.3 %collective-permute-start = (bf16[128,1152]{1,0:T(8,128)(2,1)S(1)}, bf16[128,1152]{1,0:T(8,128)(2,1)S(1)}, u32[]{:S(2)}, u32[]{:S(2)}) collective-permute-start(bf16[128,1152]{1,0:T(8,128)(2,1)S(1)} %shard_map.51), channel_id=1, source_target_pairs={{0,8},{1,9},{2,10},{3,11},{4,20},{5,21},{6,22},{7,23},{8,0},{9,1},... | collective-permute-start | bytes 884744 | tf_op jit(solution)/shard_map/ppermute | solution.py:28
  5.8 6.8 %collective-permute-start.1 = (bf16[128,1152]{1,0:T(8,128)(2,1)S(1)}, bf16[128,1152]{1,0:T(8,128)(2,1)S(1)}, u32[]{:S(2)}, u32[]{:S(2)}) collective-permute-start(bf16[128,1152]{1,0:T(8,128)(2,1)S(1)} %shard_map.52), channel_id=1, source_target_pairs={{0,16},{1,17},{2,18},{3,19},{4,12},{5,13},{6,14},{7,15},{8,24},{9,... | collective-permute-start | bytes 884744 | tf_op jit(solution)/shard_map/ppermute | solution.py:28
  7.3 17.0 %copy-start.1 = (bf16[128,1,128]{2,0,1:T(8,128)(2,1)S(1)}, bf16[128,1,128]{2,0,1:T(8,128)(2,1)}, u32[]{:S(2)}) copy-start(bf16[128,1,128]{2,0,1:T(8,128)(2,1)} %param.4) | copy-start | bytes 98308
  7.3 15.5 %collective-permute-start.5 = (f32[512,128]{1,0:T(8,128)S(1)}, f32[512,128]{1,0:T(8,128)S(1)}, u32[]{:S(2)}, u32[]{:S(2)}) collective-permute-start(f32[512,128]{1,0:T(8,128)S(1)} %bitcast.16), channel_id=1, source_target_pairs={{0,4},{1,5},{2,6},{3,7},{4,0},{5,1},{6,2},{7,3},{8,12},{9,13},{10,... | collective-permute-start | bytes 786440 | tf_op jit(solution)/shard_map/ppermute | solution.py:28
  8.4 15.9 %collective-permute-start.2 = (bf16[128,1024]{1,0:T(8,128)(2,1)S(1)}, bf16[128,1024]{1,0:T(8,128)(2,1)S(1)}, u32[]{:S(2)}, u32[]{:S(2)}) collective-permute-start(bf16[128,1024]{1,0:T(8,128)(2,1)S(1)} %shard_map.53), channel_id=1, source_target_pairs={{0,24},{1,25},{2,26},{3,27},{4,28},{5,29},{6,30},{7,31},{8,16},{9,... | collective-permute-start | bytes 786440 | tf_op jit(solution)/shard_map/ppermute | solution.py:28
  12.6 10.3 %collective-permute-start.4 = (bf16[384,128]{1,0:T(8,128)(2,1)S(1)}, bf16[384,128]{1,0:T(8,128)(2,1)S(1)}, u32[]{:S(2)}, u32[]{:S(2)}) collective-permute-start(bf16[384,128]{1,0:T(8,128)(2,1)S(1)} %pad_maximum_fusion), channel_id=1, source_target_pairs={{0,1},{1,0},{2,3},{3,2},{4,5},{5,4},{6,7},{7,6},{8,9},{9,8},{10,11... | collective-permute-start | bytes 294920 | tf_op jit(solution)/shard_map/ppermute | solution.py:28
  14.2 6.2 %collective-permute-start.3 = (bf16[128,128]{1,0:T(8,128)(2,1)S(1)}, bf16[128,128]{1,0:T(8,128)(2,1)S(1)}, u32[]{:S(2)}, u32[]{:S(2)}) collective-permute-start(bf16[128,128]{1,0:T(8,128)(2,1)S(1)} %bitcast.14), channel_id=1, source_target_pairs={{0,24},{1,25},{2,26},{3,27},{4,28},{5,29},{6,30},{7,31},{8,16},{9,... | collective-permute-start | bytes 98312 | tf_op jit(solution)/shard_map/ppermute | solution.py:28
  20.4 3.9 %collective-permute-start.6 = (bf16[128,128]{1,0:T(8,128)(2,1)S(1)}, bf16[128,128]{1,0:T(8,128)(2,1)S(1)}, u32[]{:S(2)}, u32[]{:S(2)}) collective-permute-start(bf16[128,128]{1,0:T(8,128)(2,1)S(1)} %collective-permute-done.3.refs_5_), channel_id=1, source_target_pairs={{0,1},{1,0},{2,3},{3,2},{4,5},{5,4},{6,7},{7,6},{8,9},{9,8},{10,11... | collective-permute-start | bytes 98312 | tf_op jit(solution)/shard_map/ppermute | solution.py:28
  24.8 2.0 %collective-permute-start.7 = (f32[1024,128]{1,0:T(8,128)S(1)}, f32[1024,128]{1,0:T(8,128)S(1)}, u32[]{:S(2)}, u32[]{:S(2)}) collective-permute-start(f32[1024,128]{1,0:T(8,128)S(1)} %partial.1.own_ref), channel_id=1, source_target_pairs={{0,4},{1,5},{2,6},{3,7},{4,0},{5,1},{6,2},{7,3},{8,12},{9,13},{10,... | collective-permute-start | bytes 1572872 | tf_op jit(solution)/shard_map/ppermute | solution.py:28
  27.3 4.0 %collective-permute-start.10 = (f32[72,128]{1,0:T(8,128)S(1)}, f32[72,128]{1,0:T(8,128)S(1)}, u32[]{:S(2)}, u32[]{:S(2)}) collective-permute-start(f32[72,128]{1,0:T(8,128)S(1)} %get-tuple-element.9), channel_id=1, source_target_pairs={{0,8},{1,9},{2,10},{3,11},{4,20},{5,21},{6,22},{7,23},{8,0},{9,1},... | collective-permute-start | bytes 110600 | tf_op jit(solution)/shard_map/ppermute | solution.py:28
  28.7 4.4 %collective-permute-start.9 = (f32[72,128]{1,0:T(8,128)S(1)}, f32[72,128]{1,0:T(8,128)S(1)}, u32[]{:S(2)}, u32[]{:S(2)}) collective-permute-start(f32[72,128]{1,0:T(8,128)S(1)} %get-tuple-element.9), channel_id=1, source_target_pairs={{0,16},{1,17},{2,18},{3,19},{4,12},{5,13},{6,14},{7,15},{8,24},{9,... | collective-permute-start | bytes 110600 | tf_op jit(solution)/shard_map/ppermute | solution.py:28
  29.4 4.9 %collective-permute-start.8 = (f32[72,128]{1,0:T(8,128)S(1)}, f32[72,128]{1,0:T(8,128)S(1)}, u32[]{:S(2)}, u32[]{:S(2)}) collective-permute-start(f32[72,128]{1,0:T(8,128)S(1)} %get-tuple-element.9), channel_id=1, source_target_pairs={{0,24},{1,25},{2,26},{3,27},{4,28},{5,29},{6,30},{7,31},{8,16},{9,... | collective-permute-start | bytes 110600 | tf_op jit(solution)/shard_map/ppermute | solution.py:28
  34.3 4.0 %collective-permute-start.11 = (f32[72,128]{1,0:T(8,128)S(1)}, f32[72,128]{1,0:T(8,128)S(1)}, u32[]{:S(2)}, u32[]{:S(2)}) collective-permute-start(f32[72,128]{1,0:T(8,128)S(1)} %add_add_fusion.refs_0_), channel_id=1, source_target_pairs={{0,1},{1,0},{2,3},{3,2},{4,5},{5,4},{6,7},{7,6},{8,9},{9,8},{10,11... | collective-permute-start | bytes 110600 | tf_op jit(solution)/shard_map/ppermute | solution.py:28

commit v6 on v5

--- a/solution.py
+++ b/solution.py
@@ -117,15 +117,22 @@
         copy.wait()
 
 
-def partial_kernel(n_pieces, *refs):
-    features, keys, grads_ref = refs[:n_pieces], list(refs[n_pieces:-1]), refs[-1]
+def product_sum(pieces, own, partner, head_size):
+    keys = jnp.concatenate([jnp.concatenate(own, axis=0), partner], axis=1)
+    both = lax.dot_general(jnp.concatenate(pieces, axis=0), keys, contract, preferred_element_type=jnp.float32)
+    return both[:, :head_size] + both[:, head_size:]
+
+
+def near_kernel(*refs):
+    pieces, own_ref, partner_ref, grads_ref = refs[:-3], *refs[-3:]
     rows, head_size = grads_ref.shape
-    own = [keys.pop(0)[...] if not i or far(i) else piece[:, rows:] for i, piece in enumerate(features)]
-    partner = [ref[...] for ref in keys]
-    keys = jnp.concatenate([jnp.concatenate(own, axis=0), jnp.concatenate(partner, axis=0)], axis=1)
-    features = jnp.concatenate([piece[:, :rows] for piece in features], axis=0)
-    both = lax.dot_general(features, keys, contract, preferred_element_type=jnp.float32)
-    grads_ref[...] = both[:, :head_size] + both[:, head_size:]
+    own = [own_ref[...]] + [piece[:, rows:] for piece in pieces[1:]]
+    grads_ref[...] = product_sum([piece[:, :rows] for piece in pieces], own, partner_ref[...], head_size)
+
+
+def far_kernel(near_ref, piece_ref, own_ref, partner_ref, grads_ref):
+    head_size = grads_ref.shape[1]
+    grads_ref[...] = near_ref[...] + product_sum([piece_ref[...]], [own_ref[...]], partner_ref[...], head_size)
 
 
 def joined_kernel(own_ref, other_ref, moment_ref, twin_ref, fresh_ref, blend_ref, gram_ref):
@@ -248,13 +255,24 @@
         partner_keys += [swapped(keys[d], 0, 1) for d in range(n_chip) if far(d)]
         twin = swapped(moment, 1, 0)
         partner_keys[0], twin = lax.optimization_barrier((partner_keys[0], twin))
+        total = pltpu.VMEM((2 * rows_half, head_size), jnp.float32)
+        near = [pieces[d] for d in range(n_chip) if not far(d)]
         grads = pl.pallas_call(
-            lambda *refs: partial_kernel(n_chip, *refs),
-            out_shape=pltpu.VMEM((2 * rows_half, head_size), jnp.float32),
-            in_specs=whole(n_chip + len(stages) + len(partner_keys)),
+            near_kernel,
+            out_shape=total,
+            in_specs=whole(len(near) + 2),
             out_specs=whole(1)[0],
-            name="partial",
-        )(*on_chip(*pieces, *stages, *partner_keys))
+            name="near",
+        )(*on_chip(*near, own_part, partner_keys[0]))
+        distant = [pieces[d] for d in range(n_chip) if far(d)]
+        for piece, own, partner in zip(distant, stages[1:], partner_keys[1:]):
+            grads = pl.pallas_call(
+                far_kernel,
+                out_shape=total,
+                in_specs=whole(4),
+                out_specs=whole(1)[0],
+                name="far",
+            )(*on_chip(grads, piece, own, partner))
         fresh, blend, gram = pl.pallas_call(
             joined_kernel,
             out_shape=(block, block, small),

time: 41.7 us -> 41.2 us (0.988)
  waiting for transfers between devices: 16.5 us -> 15.3 us
    ppermute x12, waiting for transfers between devices: 16.5 us -> 15.3 us  [swapped(): lax.ppermute(block, ('fsdp', 'tp'), [(i, i ^ mask) for i, mask in enumera...]
  transfers between devices with their start and end apart: 12 -> 12, of which waited for: 9 -> 9; matrix products, arithmetic and copies ran while one was open for 2% -> 2% of each run, Pallas kernels for 7% -> 8%
where the time goes in v6:
time: 41.2 us; the launch traced here: 41 us
  starting transfers between devices  15.6 us (38%)
  waiting for transfers between devices  15.3 us (37%)
  Pallas kernels  8.63 us (21%)
  between operations  0.74 us (2%)
  local copies, waits for them, and re-layouts  0.72 us (2%)
    ppermute x12, starting transfers between devices, swapped(): lax.ppermute(block, ('fsdp', 'tp'), [(i, i ^ mask) for i, mask in enumera...  15.6 us
    ppermute x12, waiting for transfers between devices, swapped(): lax.ppermute(block, ('fsdp', 'tp'), [(i, i ^ mask) for i, mask in enumera...  15.3 us
    pallas_call x4, Pallas kernels, ordered(): pl.pallas_call(lambda *refs, slots=slots: pack_kernel(rows_half, n_chip,...  4.06 us
    pallas_call x1, Pallas kernels, ordered(): pl.pallas_call(lambda *refs: newton_kernel(scale, len(grams), *refs), out...  3.23 us
  transfers between devices with their start and end apart: 12, of which 9 were waited for; matrix products, arithmetic and copies ran while one was open for 2% of the time, Pallas kernels for 8%

profile of v6, /device:TPU:0, one launch (start us, length us, event | category | flops | bytes accessed | tf_op | source)
XLA Modules:
  0.0 41.0 jit_solution(15698869021858893057)
XLA Ops:
  0.6 0.0 copy-start.2
  0.6 1.1 %shard_map.51 = bf16[128,1152]{1,0:T(8,128)(2,1)S(1)} custom-call(bf16[128,8192]{1,0:T(8,128)(2,1)} %refs_0_.7, bf16[128,128]{1,0:T(8,128)(2,1)} %bitcast.9), custom_call_target="tpu_custom_call" | custom-call | tf_op jit(solution)/shard_map/pallas_call | solution.py:237
  1.7 0.0 copy-start
  1.7 3.0 %collective-permute-start = (bf16[128,1152]{1,0:T(8,128)(2,1)S(1)}, bf16[128,1152]{1,0:T(8,128)(2,1)S(1)}, u32[]{:S(2)}, u32[]{:S(2)}) collective-permute-start(bf16[128,1152]{1,0:T(8,128)(2,1)S(1)} %shard_map.51), channel_id=1, source_target_pairs={{0,8},{1,9},{2,10},{3,11},{4,20},{5,21},{6,22},{7,23},{8,0},{9,1},... | collective-permute-start | bytes 884744 | tf_op jit(solution)/shard_map/ppermute | solution.py:28
  4.7 1.0 %shard_map.52 = bf16[128,1152]{1,0:T(8,128)(2,1)S(1)} custom-call(bf16[128,8192]{1,0:T(8,128)(2,1)} %refs_0_.7, bf16[128,128]{1,0:T(8,128)(2,1)} %bitcast.10), custom_call_target="tpu_custom_call" | custom-call | tf_op jit(solution)/shard_map/pallas_call | solution.py:237
  5.8 1.6 %collective-permute-start.1 = (bf16[128,1152]{1,0:T(8,128)(2,1)S(1)}, bf16[128,1152]{1,0:T(8,128)(2,1)S(1)}, u32[]{:S(2)}, u32[]{:S(2)}) collective-permute-start(bf16[128,1152]{1,0:T(8,128)(2,1)S(1)} %shard_map.52), channel_id=1, source_target_pairs={{0,16},{1,17},{2,18},{3,19},{4,12},{5,13},{6,14},{7,15},{8,24},{9,... | collective-permute-start | bytes 884744 | tf_op jit(solution)/shard_map/ppermute | solution.py:28
  7.3 0.0 copy-done.2
  7.3 0.0 copy-start.1
  7.3 0.0 collective-permute-start.3
  7.3 1.0 %shard_map.53 = bf16[128,1024]{1,0:T(8,128)(2,1)S(1)} custom-call(bf16[128,8192]{1,0:T(8,128)(2,1)} %refs_0_.7, bf16[128,128]{1,0:T(8,128)(2,1)} %bitcast.11), custom_call_target="tpu_custom_call" | custom-call | tf_op jit(solution)/shard_map/pallas_call | solution.py:237
  8.4 0.1 collective-permute-start.4
  8.5 2.5 %collective-permute-done.refs_1_ = bf16[128,1152]{1,0:T(8,128)(2,1)S(1)} collective-permute-done((bf16[128,1152]{1,0:T(8,128)(2,1)S(1)}, bf16[128,1152]{1,0:T(8,128)(2,1)S(1)}, u32[]{:S(2)}, u32[]{:S(2)}) %collective-permute-start) | collective-permute-done | bytes 294944 | tf_op jit(solution)/shard_map/ppermute | solution.py:28
  11.0 1.6 %collective-permute-done.1.refs_2_ = bf16[128,1152]{1,0:T(8,128)(2,1)S(1)} collective-permute-done((bf16[128,1152]{1,0:T(8,128)(2,1)S(1)}, bf16[128,1152]{1,0:T(8,128)(2,1)S(1)}, u32[]{:S(2)}, u32[]{:S(2)}) %collective-permute-start.1) | collective-permute-done | bytes 294944 | tf_op jit(solution)/shard_map/ppermute | solution.py:28
  12.5 0.0 copy-done
  12.6 1.6 %collective-permute-start.2 = (bf16[384,128]{1,0:T(8,128)(2,1)S(1)}, bf16[384,128]{1,0:T(8,128)(2,1)S(1)}, u32[]{:S(2)}, u32[]{:S(2)}) collective-permute-start(bf16[384,128]{1,0:T(8,128)(2,1)S(1)} %pad_maximum_fusion), channel_id=1, source_target_pairs={{0,1},{1,0},{2,3},{3,2},{4,5},{5,4},{6,7},{7,6},{8,9},{9,8},{10,11... | collective-permute-start | bytes 294920 | tf_op jit(solution)/shard_map/ppermute | solution.py:28
  14.2 2.9 %collective-permute-start.5 = (bf16[128,128]{1,0:T(8,128)(2,1)S(1)}, bf16[128,128]{1,0:T(8,128)(2,1)S(1)}, u32[]{:S(2)}, u32[]{:S(2)}) collective-permute-start(bf16[128,128]{1,0:T(8,128)(2,1)S(1)} %bitcast.14), channel_id=1, source_target_pairs={{0,24},{1,25},{2,26},{3,27},{4,28},{5,29},{6,30},{7,31},{8,16},{9,... | collective-permute-start | bytes 98312 | tf_op jit(solution)/shard_map/ppermute | solution.py:28
  17.1 3.3 %collective-permute-done.5.own_ref = bf16[128,128]{1,0:T(8,128)(2,1)S(1)} collective-permute-done((bf16[128,128]{1,0:T(8,128)(2,1)S(1)}, bf16[128,128]{1,0:T(8,128)(2,1)S(1)}, u32[]{:S(2)}, u32[]{:S(2)}) %collective-permute-start.5) | collective-permute-done | bytes 32800 | tf_op jit(solution)/shard_map/ppermute | solution.py:28
  20.4 1.4 %collective-permute-start.6 = (bf16[128,128]{1,0:T(8,128)(2,1)S(1)}, bf16[128,128]{1,0:T(8,128)(2,1)S(1)}, u32[]{:S(2)}, u32[]{:S(2)}) collective-permute-start(bf16[128,128]{1,0:T(8,128)(2,1)S(1)} %collective-permute-done.5.own_ref), channel_id=1, source_target_pairs={{0,1},{1,0},{2,3},{3,2},{4,5},{5,4},{6,7},{7,6},{8,9},{9,8},{10,11... | collective-permute-start | bytes 98312 | tf_op jit(solution)/shard_map/ppermute | solution.py:28
  21.8 1.0 %shard_map.50.refs_0_ = bf16[128,1024]{1,0:T(8,128)(2,1)S(1)} custom-call(bf16[128,8192]{1,0:T(8,128)(2,1)} %refs_0_.7, bf16[128,128]{1,0:T(8,128)(2,1)} %bitcast.12), custom_call_target="tpu_custom_call" | custom-call | tf_op jit(solution)/shard_map/pallas_call | solution.py:237
  22.8 0.0 collective-permute-done.3.twin_ref
  22.8 0.0 collective-permute-done.2.refs_4_
  22.9 0.0 copy-done.1
  22.9 0.5 %near.1.near_ref = f32[1024,128]{1,0:T(8,128)S(1)} custom-call(bf16[128,1024]{1,0:T(8,128)(2,1)S(1)} %shard_map.50.refs_0_, bf16[128,1152]{1,0:T(8,128)(2,1)S(1)} %collective-permute-done.refs_1_, bf16[128,1152]{1,0:T(8,128)(2,1)S(1)} %collective-permute-done.1.refs_2_, bf16[128,128]{1,0:T(8,128)(2,1)S(1)} %bitcast.15, ...), custom_call_target="tpu_custom_call" | custom-call | tf_op jit(solution)/shard_map/near/pallas_call | solution.py:260
  23.3 1.0 %collective-permute-done.6.partner_ref = bf16[128,128]{1,0:T(8,128)(2,1)S(1)} collective-permute-done((bf16[128,128]{1,0:T(8,128)(2,1)S(1)}, bf16[128,128]{1,0:T(8,128)(2,1)S(1)}, u32[]{:S(2)}, u32[]{:S(2)}) %collective-permute-start.6) | collective-permute-done | bytes 32800 | tf_op jit(solution)/shard_map/ppermute | solution.py:28
  24.3 0.0 collective-permute-done.4.piece_ref
  24.3 0.3 far.1.own_ref
  24.6 0.1 collective-permute-start.7
  24.7 1.9 %collective-permute-done.7.other_ref = f32[1024,128]{1,0:T(8,128)S(1)} collective-permute-done((f32[1024,128]{1,0:T(8,128)S(1)}, f32[1024,128]{1,0:T(8,128)S(1)}, u32[]{:S(2)}, u32[]{:S(2)}) %collective-permute-start.7) | collective-permute-done | bytes 524320 | tf_op jit(solution)/shard_map/ppermute | solution.py:28
  26.6 0.5 %gradient.1 = (f32[512,128]{1,0:T(8,128)S(1)}, f32[512,128]{1,0:T(8,128)S(1)}, f32[72,128]{1,0:T(8,128)S(1)}) custom-call(f32[1024,128]{1,0:T(8,128)S(1)} %far.1.own_ref, f32[1024,128]{1,0:T(8,128)S(1)} %collective-permute-done.7.other_ref, f32[512,128]{1,0:T(8,128)S(1)} %bitcast.17, f32[512,128]{1,0:T(8,128)S(1)} %collective-permute-done.3.twin_ref), custom_call_target="tpu_custom_call" | custom-call | tf_op jit(solution)/shard_map/gradient/pallas_call | solution.py:276
  27.2 1.4 %collective-permute-start.10 = (f32[72,128]{1,0:T(8,128)S(1)}, f32[72,128]{1,0:T(8,128)S(1)}, u32[]{:S(2)}, u32[]{:S(2)}) collective-permute-start(f32[72,128]{1,0:T(8,128)S(1)} %get-tuple-element.9), channel_id=1, source_target_pairs={{0,8},{1,9},{2,10},{3,11},{4,20},{5,21},{6,22},{7,23},{8,0},{9,1},... | collective-permute-start | bytes 110600 | tf_op jit(solution)/shard_map/ppermute | solution.py:28
  28.5 0.9 %collective-permute-start.8 = (f32[72,128]{1,0:T(8,128)S(1)}, f32[72,128]{1,0:T(8,128)S(1)}, u32[]{:S(2)}, u32[]{:S(2)}) collective-permute-start(f32[72,128]{1,0:T(8,128)S(1)} %get-tuple-element.9), channel_id=1, source_target_pairs={{0,24},{1,25},{2,26},{3,27},{4,28},{5,29},{6,30},{7,31},{8,16},{9,... | collective-permute-start | bytes 110600 | tf_op jit(solution)/shard_map/ppermute | solution.py:28
  29.4 1.3 %collective-permute-start.9 = (f32[72,128]{1,0:T(8,128)S(1)}, f32[72,128]{1,0:T(8,128)S(1)}, u32[]{:S(2)}, u32[]{:S(2)}) collective-permute-start(f32[72,128]{1,0:T(8,128)S(1)} %get-tuple-element.9), channel_id=1, source_target_pairs={{0,16},{1,17},{2,18},{3,19},{4,12},{5,13},{6,14},{7,15},{8,24},{9,... | collective-permute-start | bytes 110600 | tf_op jit(solution)/shard_map/ppermute | solution.py:28
  30.6 0.5 %collective-permute-done.10 = f32[72,128]{1,0:T(8,128)S(1)} collective-permute-done((f32[72,128]{1,0:T(8,128)S(1)}, f32[72,128]{1,0:T(8,128)S(1)}, u32[]{:S(2)}, u32[]{:S(2)}) %collective-permute-start.10) | collective-permute-done | bytes 36896 | tf_op jit(solution)/shard_map/ppermute | solution.py:28
  31.2 2.3 %collective-permute-done.8 = f32[72,128]{1,0:T(8,128)S(1)} collective-permute-done((f32[72,128]{1,0:T(8,128)S(1)}, f32[72,128]{1,0:T(8,128)S(1)}, u32[]{:S(2)}, u32[]{:S(2)}) %collective-permute-start.8) | collective-permute-done | bytes 36896 | tf_op jit(solution)/shard_map/ppermute | solution.py:28
  33.5 0.3 collective-permute-done.9
  33.8 1.3 %collective-permute-start.11 = (f32[72,128]{1,0:T(8,128)S(1)}, f32[72,128]{1,0:T(8,128)S(1)}, u32[]{:S(2)}, u32[]{:S(2)}) collective-permute-start(f32[72,128]{1,0:T(8,128)S(1)} %add_add_fusion.refs_0_), channel_id=1, source_target_pairs={{0,1},{1,0},{2,3},{3,2},{4,5},{5,4},{6,7},{7,6},{8,9},{9,8},{10,11... | collective-permute-start | bytes 110600 | tf_op jit(solution)/shard_map/ppermute | solution.py:28
  35.0 0.7 %copy.7 = f32[512,1,128]{2,1,0:T(1,128)} copy(f32[512,1,128]{2,1,0:T(1,128)S(1)} %bitcast.8) | data formatting | bytes 524288
  35.7 2.0 %collective-permute-done.11.refs_1_ = f32[72,128]{1,0:T(8,128)S(1)} collective-permute-done((f32[72,128]{1,0:T(8,128)S(1)}, f32[72,128]{1,0:T(8,128)S(1)}, u32[]{:S(2)}, u32[]{:S(2)}) %collective-permute-start.11) | collective-permute-done | bytes 36896 | tf_op jit(solution)/shard_map/ppermute | solution.py:28
  37.8 3.2 %newton.1 = f32[512,128]{1,0:T(8,128)} custom-call(f32[72,128]{1,0:T(8,128)S(1)} %add_add_fusion.refs_0_, f32[72,128]{1,0:T(8,128)S(1)} %collective-permute-done.11.refs_1_, f32[512,128]{1,0:T(8,128)S(1)} %get-tuple-element.10.refs_2_), custom_call_target="tpu_custom_call" | custom-call | tf_op jit(solution)/shard_map/newton/pallas_call | solution.py:309
  (4 shorter events, 0.0 us)
Async XLA Ops:
  0.6 6.7 %copy-start.2 = (f32[512,1,128]{2,1,0:T(1,128)S(1)}, f32[512,1,128]{2,1,0:T(1,128)}, u32[]{:S(2)}) copy-start(f32[512,1,128]{2,1,0:T(1,128)} %param.5) | copy-start | bytes 786436
  1.7 10.8 %copy-start = (bf16[128,1,128]{2,0,1:T(8,128)(2,1)S(1)}, bf16[128,1,128]{2,0,1:T(8,128)(2,1)}, u32[]{:S(2)}) copy-start(bf16[128,1,128]{2,0,1:T(8,128)(2,1)} %param.4) | copy-start | bytes 98308
  1.7 9.3 %collective-permute-start = (bf16[128,1152]{1,0:T(8,128)(2,1)S(1)}, bf16[128,1152]{1,0:T(8,128)(2,1)S(1)}, u32[]{:S(2)}, u32[]{:S(2)}) collective-permute-start(bf16[128,1152]{1,0:T(8,128)(2,1)S(1)} %shard_map.51), channel_id=1, source_target_pairs={{0,8},{1,9},{2,10},{3,11},{4,20},{5,21},{6,22},{7,23},{8,0},{9,1},... | collective-permute-start | bytes 884744 | tf_op jit(solution)/shard_map/ppermute | solution.py:28
  5.8 6.8 %collective-permute-start.1 = (bf16[128,1152]{1,0:T(8,128)(2,1)S(1)}, bf16[128,1152]{1,0:T(8,128)(2,1)S(1)}, u32[]{:S(2)}, u32[]{:S(2)}) collective-permute-start(bf16[128,1152]{1,0:T(8,128)(2,1)S(1)} %shard_map.52), channel_id=1, source_target_pairs={{0,16},{1,17},{2,18},{3,19},{4,12},{5,13},{6,14},{7,15},{8,24},{9,... | collective-permute-start | bytes 884744 | tf_op jit(solution)/shard_map/ppermute | solution.py:28
  7.3 15.5 %copy-start.1 = (bf16[128,1,128]{2,0,1:T(8,128)(2,1)S(1)}, bf16[128,1,128]{2,0,1:T(8,128)(2,1)}, u32[]{:S(2)}) copy-start(bf16[128,1,128]{2,0,1:T(8,128)(2,1)} %param.4) | copy-start | bytes 98308
  7.3 15.5 %collective-permute-start.3 = (f32[512,128]{1,0:T(8,128)S(1)}, f32[512,128]{1,0:T(8,128)S(1)}, u32[]{:S(2)}, u32[]{:S(2)}) collective-permute-start(f32[512,128]{1,0:T(8,128)S(1)} %bitcast.16), channel_id=1, source_target_pairs={{0,4},{1,5},{2,6},{3,7},{4,0},{5,1},{6,2},{7,3},{8,12},{9,13},{10,... | collective-permute-start | bytes 786440 | tf_op jit(solution)/shard_map/ppermute | solution.py:28
  8.4 15.9 %collective-permute-start.4 = (bf16[128,1024]{1,0:T(8,128)(2,1)S(1)}, bf16[128,1024]{1,0:T(8,128)(2,1)S(1)}, u32[]{:S(2)}, u32[]{:S(2)}) collective-permute-start(bf16[128,1024]{1,0:T(8,128)(2,1)S(1)} %shard_map.53), channel_id=1, source_target_pairs={{0,24},{1,25},{2,26},{3,27},{4,28},{5,29},{6,30},{7,31},{8,16},{9,... | collective-permute-start | bytes 786440 | tf_op jit(solution)/shard_map/ppermute | solution.py:28
  12.6 10.3 %collective-permute-start.2 = (bf16[384,128]{1,0:T(8,128)(2,1)S(1)}, bf16[384,128]{1,0:T(8,128)(2,1)S(1)}, u32[]{:S(2)}, u32[]{:S(2)}) collective-permute-start(bf16[384,128]{1,0:T(8,128)(2,1)S(1)} %pad_maximum_fusion), channel_id=1, source_target_pairs={{0,1},{1,0},{2,3},{3,2},{4,5},{5,4},{6,7},{7,6},{8,9},{9,8},{10,11... | collective-permute-start | bytes 294920 | tf_op jit(solution)/shard_map/ppermute | solution.py:28
  14.2 6.2 %collective-permute-start.5 = (bf16[128,128]{1,0:T(8,128)(2,1)S(1)}, bf16[128,128]{1,0:T(8,128)(2,1)S(1)}, u32[]{:S(2)}, u32[]{:S(2)}) collective-permute-start(bf16[128,128]{1,0:T(8,128)(2,1)S(1)} %bitcast.14), channel_id=1, source_target_pairs={{0,24},{1,25},{2,26},{3,27},{4,28},{5,29},{6,30},{7,31},{8,16},{9,... | collective-permute-start | bytes 98312 | tf_op jit(solution)/shard_map/ppermute | solution.py:28
  20.4 3.9 %collective-permute-start.6 = (bf16[128,128]{1,0:T(8,128)(2,1)S(1)}, bf16[128,128]{1,0:T(8,128)(2,1)S(1)}, u32[]{:S(2)}, u32[]{:S(2)}) collective-permute-start(bf16[128,128]{1,0:T(8,128)(2,1)S(1)} %collective-permute-done.5.own_ref), channel_id=1, source_target_pairs={{0,1},{1,0},{2,3},{3,2},{4,5},{5,4},{6,7},{7,6},{8,9},{9,8},{10,11... | collective-permute-start | bytes 98312 | tf_op jit(solution)/shard_map/ppermute | solution.py:28
  24.6 2.0 %collective-permute-start.7 = (f32[1024,128]{1,0:T(8,128)S(1)}, f32[1024,128]{1,0:T(8,128)S(1)}, u32[]{:S(2)}, u32[]{:S(2)}) collective-permute-start(f32[1024,128]{1,0:T(8,128)S(1)} %far.1.own_ref), channel_id=1, source_target_pairs={{0,4},{1,5},{2,6},{3,7},{4,0},{5,1},{6,2},{7,3},{8,12},{9,13},{10,... | collective-permute-start | bytes 1572872 | tf_op jit(solution)/shard_map/ppermute | solution.py:28
  27.2 4.0 %collective-permute-start.10 = (f32[72,128]{1,0:T(8,128)S(1)}, f32[72,128]{1,0:T(8,128)S(1)}, u32[]{:S(2)}, u32[]{:S(2)}) collective-permute-start(f32[72,128]{1,0:T(8,128)S(1)} %get-tuple-element.9), channel_id=1, source_target_pairs={{0,8},{1,9},{2,10},{3,11},{4,20},{5,21},{6,22},{7,23},{8,0},{9,1},... | collective-permute-start | bytes 110600 | tf_op jit(solution)/shard_map/ppermute | solution.py:28
  28.5 5.0 %collective-permute-start.8 = (f32[72,128]{1,0:T(8,128)S(1)}, f32[72,128]{1,0:T(8,128)S(1)}, u32[]{:S(2)}, u32[]{:S(2)}) collective-permute-start(f32[72,128]{1,0:T(8,128)S(1)} %get-tuple-element.9), channel_id=1, source_target_pairs={{0,24},{1,25},{2,26},{3,27},{4,28},{5,29},{6,30},{7,31},{8,16},{9,... | collective-permute-start | bytes 110600 | tf_op jit(solution)/shard_map/ppermute | solution.py:28
  29.4 4.4 %collective-permute-start.9 = (f32[72,128]{1,0:T(8,128)S(1)}, f32[72,128]{1,0:T(8,128)S(1)}, u32[]{:S(2)}, u32[]{:S(2)}) collective-permute-start(f32[72,128]{1,0:T(8,128)S(1)} %get-tuple-element.9), channel_id=1, source_target_pairs={{0,16},{1,17},{2,18},{3,19},{4,12},{5,13},{6,14},{7,15},{8,24},{9,... | collective-permute-start | bytes 110600 | tf_op jit(solution)/shard_map/ppermute | solution.py:28
  33.8 4.0 %collective-permute-start.11 = (f32[72,128]{1,0:T(8,128)S(1)}, f32[72,128]{1,0:T(8,128)S(1)}, u32[]{:S(2)}, u32[]{:S(2)}) collective-permute-start(f32[72,128]{1,0:T(8,128)S(1)} %add_add_fusion.refs_0_), channel_id=1, source_target_pairs={{0,1},{1,0},{2,3},{3,2},{4,5},{5,4},{6,7},{7,6},{8,9},{9,8},{10,11... | collective-permute-start | bytes 110600 | tf_op jit(solution)/shard_map/ppermute | solution.py:28
